TPU v7x, 32 devices: a whole 2x2x4 slice. The times are simulated.
32 devices in a mesh: section: 4 (over y, x), tile: 8 (over z, core).
Axes of the slice: x: 2, y: 2, z: 4, core: 2. Of those that a mesh axis runs over, the one named last changes fastest.
Arguments:
- hidden: bfloat16 [512, 2560], P('tile'), may hold values from -110 to 110
- keys_values: bfloat16 [4, 512, 2, 2560], P('section', 'tile'), may hold values from -60 to 60
- q_gain: float32 [4, 2560], P('section'), may hold values from 0.1 to 1.9
- tile_mask: int32 [8, 7], P('tile'), may hold values from 0 to 1, as said below
Outputs:
- attended: bfloat16 [4, 512, 2560], P('section', 'tile')
Inputs may be any that keep to these rules, and one draw needn't show every extreme that they name: tile_mask[i, 3] is 1 for every tile; entries whose tile lies outside 0 to 7 are 0.
All inputs are finite; a program needn't handle non-finite values.
Results may differ from a plain program's by a relative error of at most 0.013.
Values may be sent and summed in bfloat16 or wider, within the bound.
No kernel may reach another device: no remote copies, remote signals or barrier semaphores. Data moves between devices by JAX's collectives and lax.ppermute only.
A program may use at most 64 MiB of HBM per device.

v0:
```python
import functools

import jax
import jax.numpy as jnp
from jax import lax
from jax.experimental import pallas as pl
from jax.experimental.pallas import tpu as pltpu
from jax.sharding import PartitionSpec as P


HD = 128
WIN = 3
LANES = 128
NEG = -1e30
LOG2E = 1.4426950408889634
PIECES = 2
SLOTS = (0, 2, -2, -3, 1, -1, 3)
ATTEND_VMEM = 24 << 20
SPLIT_VMEM = 8 << 20


def vmem():
    return pl.BlockSpec(memory_space=pltpu.VMEM)


def smem():
    return pl.BlockSpec(memory_space=pltpu.SMEM)


def split_body(kv_ref, out_ref):
    rows = kv_ref.shape[0]
    i = lax.broadcasted_iota(jnp.int32, (2 * rows, 2 * rows), 0)
    j = lax.broadcasted_iota(jnp.int32, (2 * rows, 2 * rows), 1)
    source = jnp.where(i < rows, 2 * i, 2 * (i - rows) + 1)
    sort = jnp.where(j == source, 1.0, 0.0).astype(jnp.bfloat16)
    for c in range(0, kv_ref.shape[2], HD):
        mixed = kv_ref[:, :, c : c + HD].reshape(2 * rows, HD)
        both = jnp.dot(sort, mixed, preferred_element_type=jnp.float32).astype(jnp.bfloat16)
        out_ref[0, :, c : c + HD] = both[:rows]
        out_ref[1, :, c : c + HD] = both[rows:]


def split_keys_values(kv):
    rows, _, channels = kv.shape
    return pl.pallas_call(
        split_body,
        out_shape=jax.ShapeDtypeStruct((2, rows, channels), jnp.bfloat16),
        in_specs=[vmem()],
        out_specs=vmem(),
        compiler_params=pltpu.CompilerParams(vmem_limit_bytes=SPLIT_VMEM),
        name="split_kv",
    )(kv)


def attend_rows(mask_ref, src_ref, rows, gain_ref, tile_refs):
    count = rows.stop - rows.start
    channels = src_ref.shape[1]
    tile_rows = tile_refs[0].shape[1]
    keys = len(tile_refs) * tile_rows
    heads = LANES // count
    width = heads * HD
    sign = 1 - 2 * (lax.axis_index("tile") % 2)
    x = src_ref[rows, :].astype(jnp.float32)
    inv = lax.rsqrt(jnp.mean(x * x, axis=-1, keepdims=True) + 1e-06)
    key = lax.broadcasted_iota(jnp.int32, (keys, LANES), 0)
    bias = jnp.full((keys, LANES), NEG, jnp.float32)
    for s, offset in enumerate(SLOTS):
        bit = mask_ref[0, WIN + sign * offset]
        here = (key >= s * tile_rows) & (key < (s + 1) * tile_rows) & (bit > 0)
        bias = jnp.where(here, 0.0, bias)
    zero = jnp.zeros((count, HD), jnp.bfloat16)
    groups = [slice(c, c + width) for c in range(0, channels, width)]
    states = [src_ref[rows, g].astype(jnp.float32) for g in groups]
    queries = []
    for g, state in zip(groups, states):
        query = (state * inv * gain_ref[:, g]).astype(jnp.bfloat16)
        blocks = [
            jnp.concatenate(
                [query[:, b * HD : (b + 1) * HD] if a == b else zero for b in range(heads)], axis=1
            )
            for a in range(heads)
        ]
        queries.append(jnp.concatenate(blocks, axis=0))
    scores = [
        lax.dot_general(
            jnp.concatenate([t[0, :, g] for t in tile_refs], axis=0),
            query,
            (((1,), (1,)), ((), ())),
            preferred_element_type=jnp.float32,
        )
        + bias
        for g, query in zip(groups, queries)
    ]
    tops = [jnp.max(s, axis=0, keepdims=True) for s in scores]
    weights = [jnp.exp2((s - top) * (HD**-0.5 * LOG2E)) for s, top in zip(scores, tops)]
    totals = [jnp.sum(w, axis=0, keepdims=True) for w in weights]
    mixed = [
        lax.dot_general(
            w.astype(jnp.bfloat16),
            jnp.concatenate([t[1, :, g] for t in tile_refs], axis=0),
            (((0,), (0,)), ((), ())),
            preferred_element_type=jnp.float32,
        )
        for g, w in zip(groups, weights)
    ]
    done = []
    for g, state, m, total in zip(groups, states, mixed, totals):
        by_row = jnp.transpose(jnp.broadcast_to(total, (LANES, LANES)))
        result = jnp.concatenate(
            [
                m[b * count : (b + 1) * count, b * HD : (b + 1) * HD]
                / by_row[b * count : (b + 1) * count]
                for b in range(heads)
            ],
            axis=1,
        ).astype(jnp.bfloat16)
        done.append((g, state, result))
    return done


def attend_body(moment, has_next, rows, mask_ref, src_ref, gain_ref, *refs):
    tile_refs = refs[: len(SLOTS)]
    rest = list(refs[len(SLOTS) :])
    kept_ref = rest.pop(0) if moment else None
    out_ref = rest.pop(0)
    next_ref = rest.pop(0) if has_next else None
    live = lax.axis_index("section") == moment

    @pl.when(live)
    def _():
        for g, state, result in attend_rows(mask_ref, src_ref, rows, gain_ref, tile_refs):
            out_ref[:, g] = result
            if has_next:
                next_ref[:, g] = (state + result.astype(jnp.float32)).astype(jnp.bfloat16)

    if kept_ref is not None:

        @pl.when(jnp.logical_not(live))
        def _():
            out_ref[...] = kept_ref[...]


def attend(moment, has_next, rows, mask, source, gain, tiles, kept):
    count = rows.stop - rows.start
    channels = source.shape[1]
    shape = jax.ShapeDtypeStruct((count, channels), jnp.bfloat16)
    keys = len(tiles) * tiles[0].shape[1]
    operands = [mask, source, gain, *tiles] + ([kept] if moment else [])
    outputs = 2 if has_next else 1
    return pl.pallas_call(
        functools.partial(attend_body, moment, has_next, rows),
        out_shape=(shape,) * outputs,
        in_specs=[smem()] + [vmem()] * (len(operands) - 1),
        out_specs=(vmem(),) * outputs,
        compiler_params=pltpu.CompilerParams(vmem_limit_bytes=ATTEND_VMEM),
        cost_estimate=pl.CostEstimate(
            flops=4 * count * keys * channels,
            bytes_accessed=4 * keys * channels + 6 * count * channels,
            transcendentals=count * keys * channels // HD,
        ),
        name="attend",
    )(*operands)


def exchange(own, tiles):
    odd = range(1, tiles, 2)
    even = range(0, tiles, 2)

    def inside(pairs):
        return [(i, j) for i, j in pairs if 0 <= j < tiles]

    def move(tile, pairs):
        return lax.ppermute(tile, "tile", pairs)

    swap = inside([(i, i ^ 1) for i in range(tiles)])
    relay = inside([(i, i + 1) for i in odd] + [(i, i - 1) for i in even])
    outward = inside([(i, i + 2) for i in odd] + [(i, i - 2) for i in even])
    first = move(own, outward)
    partner = move(own, swap)
    second = move(own, [(j, i) for i, j in outward])
    far = move(first, relay)
    partner_first = move(first, swap)
    partner_second = move(second, swap)
    return [own, first, second, far, partner, partner_first, partner_second]


def on_device(hidden, keys_values, q_gain, tile_mask):
    sections = lax.axis_size("section")
    rows = hidden.shape[0]
    count = rows // PIECES
    own = split_keys_values(keys_values[0])
    window = exchange(own, lax.axis_size("tile"))
    sources = [(hidden, slice(p * count, (p + 1) * count)) for p in range(PIECES)]
    kept = [None] * PIECES
    for moment in range(sections):
        has_next = moment + 1 < sections
        for p, (source, span) in enumerate(sources):
            results = attend(moment, has_next, span, tile_mask, source, q_gain, window, kept[p])
            kept[p] = results[0]
            if has_next:
                arrived = lax.ppermute(results[1], "section", [(moment, moment + 1)])
                sources[p] = (arrived, slice(0, count))
    attended = kept[0] if PIECES == 1 else jnp.concatenate(kept, axis=0)
    return attended[None]


def solution(mesh):
    in_specs = (
        P("tile", None),
        P("section", "tile", None, None),
        P("section", None),
        P("tile", None),
    )
    out_specs = P("section", "tile", None)
    return jax.shard_map(
        on_device, mesh=mesh, in_specs=in_specs, out_specs=out_specs, check_vma=False
    )
```

profile of v0, /device:TPU:14, one launch (start us, length us, event | category | flops | bytes accessed | tf_op | source)
XLA Modules:
  0.0 63.1 jit_solution(7797043737585668922)
XLA Ops:
  0.0 0.0 copy-start.2
  0.0 1.1 %copy-done.2 = bf16[1,64,2,2560]{3,2,1,0:T(2,128)(2,1)S(1)} copy-done((bf16[1,64,2,2560]{3,2,1,0:T(2,128)(2,1)S(1)}, bf16[1,64,2,2560]{3,2,1,0:T(2,128)(2,1)}, u32[]{:S(2)}) %copy-start.2) | copy-done | bytes 655384
  1.1 0.0 copy-start
  1.1 0.0 copy-start.1
  1.1 0.0 copy-start.3
  1.1 0.4 split_kv.1.refs_0_
  1.5 3.5 %collective-permute-start.1 = (bf16[2,64,2560]{2,1,0:T(8,128)(2,1)S(1)}, bf16[2,64,2560]{2,1,0:T(8,128)(2,1)S(1)}, u32[]{:S(2)}, u32[]{:S(2)}) collective-permute-start(bf16[2,64,2560]{2,1,0:T(8,128)(2,1)S(1)} %split_kv.1.refs_0_), channel_id=1, source_target_pairs={{3,1},{5,3},{7,5},{0,2},{2,4},{4,6},{11,9},{13,11},{15,13},{8,10},... | collective-permute-start | bytes 1966088 | tf_op jit(solution)/shard_map/ppermute | solution.py:173
  5.0 2.4 %collective-permute-start = (bf16[2,64,2560]{2,1,0:T(8,128)(2,1)S(1)}, bf16[2,64,2560]{2,1,0:T(8,128)(2,1)S(1)}, u32[]{:S(2)}, u32[]{:S(2)}) collective-permute-start(bf16[2,64,2560]{2,1,0:T(8,128)(2,1)S(1)} %split_kv.1.refs_0_), channel_id=1, source_target_pairs={{1,3},{3,5},{5,7},{2,0},{4,2},{6,4},{9,11},{11,13},{13,15},{10,8},... | collective-permute-start | bytes 1966088 | tf_op jit(solution)/shard_map/ppermute | solution.py:173
  7.4 0.1 collective-permute-start.3
  7.5 12.6 %collective-permute-done.1.refs_2_ = bf16[2,64,2560]{2,1,0:T(8,128)(2,1)S(1)} collective-permute-done((bf16[2,64,2560]{2,1,0:T(8,128)(2,1)S(1)}, bf16[2,64,2560]{2,1,0:T(8,128)(2,1)S(1)}, u32[]{:S(2)}, u32[]{:S(2)}) %collective-permute-start.1) | collective-permute-done | bytes 655392 | tf_op jit(solution)/shard_map/ppermute | solution.py:173
  20.1 0.0 collective-permute-start.5
  20.1 0.0 collective-permute-done.refs_1_
  20.1 0.8 %collective-permute-start.4 = (bf16[2,64,2560]{2,1,0:T(8,128)(2,1)S(1)}, bf16[2,64,2560]{2,1,0:T(8,128)(2,1)S(1)}, u32[]{:S(2)}, u32[]{:S(2)}) collective-permute-start(bf16[2,64,2560]{2,1,0:T(8,128)(2,1)S(1)} %collective-permute-done.refs_1_), channel_id=1, source_target_pairs={{0,1},{1,0},{2,3},{3,2},{4,5},{5,4},{6,7},{7,6},{8,9},{9,8},{10,11... | collective-permute-start | bytes 1966088 | tf_op jit(solution)/shard_map/ppermute | solution.py:173
  20.9 1.9 %collective-permute-start.2 = (bf16[2,64,2560]{2,1,0:T(8,128)(2,1)S(1)}, bf16[2,64,2560]{2,1,0:T(8,128)(2,1)S(1)}, u32[]{:S(2)}, u32[]{:S(2)}) collective-permute-start(bf16[2,64,2560]{2,1,0:T(8,128)(2,1)S(1)} %collective-permute-done.refs_1_), channel_id=1, source_target_pairs={{1,2},{3,4},{5,6},{2,1},{4,3},{6,5},{9,10},{11,12},{13,14},{10,9},... | collective-permute-start | bytes 1966088 | tf_op jit(solution)/shard_map/ppermute | solution.py:173
  22.8 0.0 collective-permute-done.3.refs_4_
  22.8 0.0 collective-permute-done.5.refs_6_
  22.8 0.3 collective-permute-done.4.refs_5_
  23.1 9.6 %collective-permute-done.2.refs_3_ = bf16[2,64,2560]{2,1,0:T(8,128)(2,1)S(1)} collective-permute-done((bf16[2,64,2560]{2,1,0:T(8,128)(2,1)S(1)}, bf16[2,64,2560]{2,1,0:T(8,128)(2,1)S(1)}, u32[]{:S(2)}, u32[]{:S(2)}) %collective-permute-start.2) | collective-permute-done | bytes 655392 | tf_op jit(solution)/shard_map/ppermute | solution.py:173
  32.8 0.0 copy-done
  32.8 0.0 copy-done.1
  32.8 0.0 copy-done.3
  32.8 0.6 attend.12
  33.3 0.7 %collective-permute-start.9 = (bf16[32,2560]{1,0:T(8,128)(2,1)S(1)}, bf16[32,2560]{1,0:T(8,128)(2,1)S(1)}, u32[]{:S(2)}, u32[]{:S(2)}) collective-permute-start(bf16[32,2560]{1,0:T(8,128)(2,1)S(1)} %get-tuple-element.23), channel_id=1, source_target_pairs={{0,8},{1,9},{2,10},{3,11},{4,12},{5,13},{6,14},{7,15}} | collective-permute-start | bytes 491528 | tf_op jit(solution)/shard_map/ppermute | solution.py:201
  34.0 0.6 attend.8
  34.6 0.7 %collective-permute-start.6 = (bf16[32,2560]{1,0:T(8,128)(2,1)S(1)}, bf16[32,2560]{1,0:T(8,128)(2,1)S(1)}, u32[]{:S(2)}, u32[]{:S(2)}) collective-permute-start(bf16[32,2560]{1,0:T(8,128)(2,1)S(1)} %get-tuple-element.17), channel_id=1, source_target_pairs={{0,8},{1,9},{2,10},{3,11},{4,12},{5,13},{6,14},{7,15}} | collective-permute-start | bytes 491528 | tf_op jit(solution)/shard_map/ppermute | solution.py:201
  35.3 0.0 collective-permute-done.9.src_ref
  35.3 0.6 attend.13
  35.8 0.7 %collective-permute-start.10 = (bf16[32,2560]{1,0:T(8,128)(2,1)S(1)}, bf16[32,2560]{1,0:T(8,128)(2,1)S(1)}, u32[]{:S(2)}, u32[]{:S(2)}) collective-permute-start(bf16[32,2560]{1,0:T(8,128)(2,1)S(1)} %get-tuple-element.25), channel_id=1, source_target_pairs={{8,16},{9,17},{10,18},{11,19},{12,20},{13,21},{14,22},{15,23}} | collective-permute-start | bytes 491528 | tf_op jit(solution)/shard_map/ppermute | solution.py:201
  36.5 0.0 collective-permute-done.6.src_ref
  36.5 0.6 attend.9
  37.1 0.7 %collective-permute-start.7 = (bf16[32,2560]{1,0:T(8,128)(2,1)S(1)}, bf16[32,2560]{1,0:T(8,128)(2,1)S(1)}, u32[]{:S(2)}, u32[]{:S(2)}) collective-permute-start(bf16[32,2560]{1,0:T(8,128)(2,1)S(1)} %get-tuple-element.19), channel_id=1, source_target_pairs={{8,16},{9,17},{10,18},{11,19},{12,20},{13,21},{14,22},{15,23}} | collective-permute-start | bytes 491528 | tf_op jit(solution)/shard_map/ppermute | solution.py:201
  37.8 0.0 collective-permute-done.10.src_ref
  37.8 0.6 attend.14
  38.4 1.3 %collective-permute-start.11 = (bf16[32,2560]{1,0:T(8,128)(2,1)S(1)}, bf16[32,2560]{1,0:T(8,128)(2,1)S(1)}, u32[]{:S(2)}, u32[]{:S(2)}) collective-permute-start(bf16[32,2560]{1,0:T(8,128)(2,1)S(1)} %get-tuple-element.27), channel_id=1, source_target_pairs={{16,24},{17,25},{18,26},{19,27},{20,28},{21,29},{22,30},{23,31}} | collective-permute-start | bytes 491528 | tf_op jit(solution)/shard_map/ppermute | solution.py:201
  39.7 0.0 collective-permute-done.7.src_ref
  39.7 0.6 attend.10
  40.3 1.3 %collective-permute-start.8 = (bf16[32,2560]{1,0:T(8,128)(2,1)S(1)}, bf16[32,2560]{1,0:T(8,128)(2,1)S(1)}, u32[]{:S(2)}, u32[]{:S(2)}) collective-permute-start(bf16[32,2560]{1,0:T(8,128)(2,1)S(1)} %get-tuple-element.21), channel_id=1, source_target_pairs={{16,24},{17,25},{18,26},{19,27},{20,28},{21,29},{22,30},{23,31}} | collective-permute-start | bytes 491528 | tf_op jit(solution)/shard_map/ppermute | solution.py:201
  41.6 15.1 %collective-permute-done.11.src_ref = bf16[32,2560]{1,0:T(8,128)(2,1)S(1)} collective-permute-done((bf16[32,2560]{1,0:T(8,128)(2,1)S(1)}, bf16[32,2560]{1,0:T(8,128)(2,1)S(1)}, u32[]{:S(2)}, u32[]{:S(2)}) %collective-permute-start.11) | collective-permute-done | bytes 163872 | tf_op jit(solution)/shard_map/ppermute | solution.py:201
  56.6 1.8 %attend.15 = bf16[32,2560]{1,0:T(8,128)(2,1)S(1)} custom-call(s32[1,7]{1,0:T(1,128)S(1)} %copy-done.3, bf16[32,2560]{1,0:T(8,128)(2,1)S(1)} %collective-permute-done.11.src_ref, f32[1,2560]{1,0:T(1,128)S(1)} %copy-done.1, bf16[2,64,2560]{2,1,0:T(8,128)(2,1)S(1)} %split_kv.1.refs_0_, bf16[2,64,2560]{2,1,0:T(8,128)(2,1)S(1)} %collective-permute-done.refs_1_, ...), custom_call_target="tpu_custom_call" | custom-call | flops 146800640 | bytes 5079040 | tf_op jit(solution)/shard_map/attend/pallas_call | solution.py:150
  58.5 2.1 %collective-permute-done.8.src_ref = bf16[32,2560]{1,0:T(8,128)(2,1)S(1)} collective-permute-done((bf16[32,2560]{1,0:T(8,128)(2,1)S(1)}, bf16[32,2560]{1,0:T(8,128)(2,1)S(1)}, u32[]{:S(2)}, u32[]{:S(2)}) %collective-permute-start.8) | collective-permute-done | bytes 163872 | tf_op jit(solution)/shard_map/ppermute | solution.py:201
  60.5 1.8 %attend.11 = bf16[32,2560]{1,0:T(8,128)(2,1)S(1)} custom-call(s32[1,7]{1,0:T(1,128)S(1)} %copy-done.3, bf16[32,2560]{1,0:T(8,128)(2,1)S(1)} %collective-permute-done.8.src_ref, f32[1,2560]{1,0:T(1,128)S(1)} %copy-done.1, bf16[2,64,2560]{2,1,0:T(8,128)(2,1)S(1)} %split_kv.1.refs_0_, bf16[2,64,2560]{2,1,0:T(8,128)(2,1)S(1)} %collective-permute-done.refs_1_, ...), custom_call_target="tpu_custom_call" | custom-call | flops 146800640 | bytes 5079040 | tf_op jit(solution)/shard_map/attend/pallas_call | solution.py:150
  62.4 0.7 %maximum_bitcast_fusion = bf16[1,64,2560]{2,1,0:T(8,128)(2,1)} fusion(bf16[32,2560]{1,0:T(8,128)(2,1)S(1)} %attend.15, bf16[32,2560]{1,0:T(8,128)(2,1)S(1)} %attend.11), kind=kLoop, calls=%fused_computation | loop fusion | flops 655360 | bytes 655360 | tf_op jit(solution)/shard_map/broadcast_in_dim | solution.py:204
Async XLA Ops:
  0.0 1.1 %copy-start.2 = (bf16[1,64,2,2560]{3,2,1,0:T(2,128)(2,1)S(1)}, bf16[1,64,2,2560]{3,2,1,0:T(2,128)(2,1)}, u32[]{:S(2)}) copy-start(bf16[1,64,2,2560]{3,2,1,0:T(2,128)(2,1)} %param.5) | copy-start | bytes 1966084
  1.1 31.7 %copy-start = (bf16[64,2560]{1,0:T(8,128)(2,1)S(1)}, bf16[64,2560]{1,0:T(8,128)(2,1)}, u32[]{:S(2)}) copy-start(bf16[64,2560]{1,0:T(8,128)(2,1)} %src_ref.3) | copy-start | bytes 983044
  1.1 31.7 %copy-start.1 = (f32[1,2560]{1,0:T(1,128)S(1)}, f32[1,2560]{1,0:T(1,128)}, u32[]{:S(2)}) copy-start(f32[1,2560]{1,0:T(1,128)} %gain_ref.15) | copy-start | bytes 30724
  1.1 31.7 %copy-start.3 = (s32[1,7]{1,0:T(1,128)S(1)}, s32[1,7]{1,0:T(1,128)}, u32[]{:S(2)}) copy-start(s32[1,7]{1,0:T(1,128)} %mask_ref.15) | copy-start | bytes 88
  1.5 18.5 %collective-permute-start.1 = (bf16[2,64,2560]{2,1,0:T(8,128)(2,1)S(1)}, bf16[2,64,2560]{2,1,0:T(8,128)(2,1)S(1)}, u32[]{:S(2)}, u32[]{:S(2)}) collective-permute-start(bf16[2,64,2560]{2,1,0:T(8,128)(2,1)S(1)} %split_kv.1.refs_0_), channel_id=1, source_target_pairs={{3,1},{5,3},{7,5},{0,2},{2,4},{4,6},{11,9},{13,11},{15,13},{8,10},... | collective-permute-start | bytes 1966088 | tf_op jit(solution)/shard_map/ppermute | solution.py:173
  5.0 15.1 %collective-permute-start = (bf16[2,64,2560]{2,1,0:T(8,128)(2,1)S(1)}, bf16[2,64,2560]{2,1,0:T(8,128)(2,1)S(1)}, u32[]{:S(2)}, u32[]{:S(2)}) collective-permute-start(bf16[2,64,2560]{2,1,0:T(8,128)(2,1)S(1)} %split_kv.1.refs_0_), channel_id=1, source_target_pairs={{1,3},{3,5},{5,7},{2,0},{4,2},{6,4},{9,11},{11,13},{13,15},{10,8},... | collective-permute-start | bytes 1966088 | tf_op jit(solution)/shard_map/ppermute | solution.py:173
  7.4 15.3 %collective-permute-start.3 = (bf16[2,64,2560]{2,1,0:T(8,128)(2,1)S(1)}, bf16[2,64,2560]{2,1,0:T(8,128)(2,1)S(1)}, u32[]{:S(2)}, u32[]{:S(2)}) collective-permute-start(bf16[2,64,2560]{2,1,0:T(8,128)(2,1)S(1)} %split_kv.1.refs_0_), channel_id=1, source_target_pairs={{0,1},{1,0},{2,3},{3,2},{4,5},{5,4},{6,7},{7,6},{8,9},{9,8},{10,11... | collective-permute-start | bytes 1966088 | tf_op jit(solution)/shard_map/ppermute | solution.py:173
  20.1 2.7 %collective-permute-start.5 = (bf16[2,64,2560]{2,1,0:T(8,128)(2,1)S(1)}, bf16[2,64,2560]{2,1,0:T(8,128)(2,1)S(1)}, u32[]{:S(2)}, u32[]{:S(2)}) collective-permute-start(bf16[2,64,2560]{2,1,0:T(8,128)(2,1)S(1)} %collective-permute-done.1.refs_2_), channel_id=1, source_target_pairs={{0,1},{1,0},{2,3},{3,2},{4,5},{5,4},{6,7},{7,6},{8,9},{9,8},{10,11... | collective-permute-start | bytes 1966088 | tf_op jit(solution)/shard_map/ppermute | solution.py:173
  20.1 3.0 %collective-permute-start.4 = (bf16[2,64,2560]{2,1,0:T(8,128)(2,1)S(1)}, bf16[2,64,2560]{2,1,0:T(8,128)(2,1)S(1)}, u32[]{:S(2)}, u32[]{:S(2)}) collective-permute-start(bf16[2,64,2560]{2,1,0:T(8,128)(2,1)S(1)} %collective-permute-done.refs_1_), channel_id=1, source_target_pairs={{0,1},{1,0},{2,3},{3,2},{4,5},{5,4},{6,7},{7,6},{8,9},{9,8},{10,11... | collective-permute-start | bytes 1966088 | tf_op jit(solution)/shard_map/ppermute | solution.py:173
  20.9 11.9 %collective-permute-start.2 = (bf16[2,64,2560]{2,1,0:T(8,128)(2,1)S(1)}, bf16[2,64,2560]{2,1,0:T(8,128)(2,1)S(1)}, u32[]{:S(2)}, u32[]{:S(2)}) collective-permute-start(bf16[2,64,2560]{2,1,0:T(8,128)(2,1)S(1)} %collective-permute-done.refs_1_), channel_id=1, source_target_pairs={{1,2},{3,4},{5,6},{2,1},{4,3},{6,5},{9,10},{11,12},{13,14},{10,9},... | collective-permute-start | bytes 1966088 | tf_op jit(solution)/shard_map/ppermute | solution.py:173
  33.3 1.9 %collective-permute-start.9 = (bf16[32,2560]{1,0:T(8,128)(2,1)S(1)}, bf16[32,2560]{1,0:T(8,128)(2,1)S(1)}, u32[]{:S(2)}, u32[]{:S(2)}) collective-permute-start(bf16[32,2560]{1,0:T(8,128)(2,1)S(1)} %get-tuple-element.23), channel_id=1, source_target_pairs={{0,8},{1,9},{2,10},{3,11},{4,12},{5,13},{6,14},{7,15}} | collective-permute-start | bytes 491528 | tf_op jit(solution)/shard_map/ppermute | solution.py:201
  34.6 1.9 %collective-permute-start.6 = (bf16[32,2560]{1,0:T(8,128)(2,1)S(1)}, bf16[32,2560]{1,0:T(8,128)(2,1)S(1)}, u32[]{:S(2)}, u32[]{:S(2)}) collective-permute-start(bf16[32,2560]{1,0:T(8,128)(2,1)S(1)} %get-tuple-element.17), channel_id=1, source_target_pairs={{0,8},{1,9},{2,10},{3,11},{4,12},{5,13},{6,14},{7,15}} | collective-permute-start | bytes 491528 | tf_op jit(solution)/shard_map/ppermute | solution.py:201
  35.8 1.9 %collective-permute-start.10 = (bf16[32,2560]{1,0:T(8,128)(2,1)S(1)}, bf16[32,2560]{1,0:T(8,128)(2,1)S(1)}, u32[]{:S(2)}, u32[]{:S(2)}) collective-permute-start(bf16[32,2560]{1,0:T(8,128)(2,1)S(1)} %get-tuple-element.25), channel_id=1, source_target_pairs={{8,16},{9,17},{10,18},{11,19},{12,20},{13,21},{14,22},{15,23}} | collective-permute-start | bytes 491528 | tf_op jit(solution)/shard_map/ppermute | solution.py:201
  37.1 2.6 %collective-permute-start.7 = (bf16[32,2560]{1,0:T(8,128)(2,1)S(1)}, bf16[32,2560]{1,0:T(8,128)(2,1)S(1)}, u32[]{:S(2)}, u32[]{:S(2)}) collective-permute-start(bf16[32,2560]{1,0:T(8,128)(2,1)S(1)} %get-tuple-element.19), channel_id=1, source_target_pairs={{8,16},{9,17},{10,18},{11,19},{12,20},{13,21},{14,22},{15,23}} | collective-permute-start | bytes 491528 | tf_op jit(solution)/shard_map/ppermute | solution.py:201
  38.4 18.2 %collective-permute-start.11 = (bf16[32,2560]{1,0:T(8,128)(2,1)S(1)}, bf16[32,2560]{1,0:T(8,128)(2,1)S(1)}, u32[]{:S(2)}, u32[]{:S(2)}) collective-permute-start(bf16[32,2560]{1,0:T(8,128)(2,1)S(1)} %get-tuple-element.27), channel_id=1, source_target_pairs={{16,24},{17,25},{18,26},{19,27},{20,28},{21,29},{22,30},{23,31}} | collective-permute-start | bytes 491528 | tf_op jit(solution)/shard_map/ppermute | solution.py:201
  40.3 20.3 %collective-permute-start.8 = (bf16[32,2560]{1,0:T(8,128)(2,1)S(1)}, bf16[32,2560]{1,0:T(8,128)(2,1)S(1)}, u32[]{:S(2)}, u32[]{:S(2)}) collective-permute-start(bf16[32,2560]{1,0:T(8,128)(2,1)S(1)} %get-tuple-element.21), channel_id=1, source_target_pairs={{16,24},{17,25},{18,26},{19,27},{20,28},{21,29},{22,30},{23,31}} | collective-permute-start | bytes 491528 | tf_op jit(solution)/shard_map/ppermute | solution.py:201
where the time goes:
time: 63.4 us; the launch traced here: 63.1 us
  waiting for transfers between devices  39.7 us (63%)
  starting transfers between devices  13.9 us (22%)
  Pallas kernels  7.52 us (12%)
  local copies, waits for them, and re-layouts  1.1 us (2%)
  other arithmetic  0.75 us (1%)
    ppermute x6, waiting for transfers between devices, move(): return lax.ppermute(tile, 'tile', pairs)  22.5 us
    ppermute x6, waiting for transfers between devices, on_device(): arrived = lax.ppermute(results[1], 'section', [(moment, moment + 1)])  17.1 us
    ppermute x6, starting transfers between devices, move(): return lax.ppermute(tile, 'tile', pairs)  8.63 us
    pallas_call x8, Pallas kernels, attend(): pl.pallas_call(functools.partial(attend_body, moment, has_next, rows), ou...  7.07 us
    ppermute x6, starting transfers between devices, on_device(): arrived = lax.ppermute(results[1], 'section', [(moment, moment + 1)])  5.27 us
  transfers between devices with their start and end apart: 12, of which 5 were waited for; matrix products, arithmetic and copies ran while one was open for 0% of the time, Pallas kernels for 7%

commit v1 on v0

--- a/solution.py
+++ b/solution.py
@@ -52,27 +52,37 @@
     )(kv)
 
 
-def attend_rows(mask_ref, src_ref, rows, gain_ref, tile_refs):
+def bias_body(tile_rows, mask_ref, out_ref):
+    sign = 1 - 2 * (lax.axis_index("tile") % 2)
+    for s, offset in enumerate(SLOTS):
+        bit = mask_ref[0, WIN + sign * offset]
+        block = jnp.full((tile_rows, LANES), jnp.where(bit > 0, 0.0, NEG), jnp.float32)
+        out_ref[s * tile_rows : (s + 1) * tile_rows, :] = block
+
+
+def mask_bias(mask, tile_rows):
+    return pl.pallas_call(
+        functools.partial(bias_body, tile_rows),
+        out_shape=jax.ShapeDtypeStruct((len(SLOTS) * tile_rows, LANES), jnp.float32),
+        in_specs=[smem()],
+        out_specs=vmem(),
+        compiler_params=pltpu.CompilerParams(vmem_limit_bytes=SPLIT_VMEM),
+        name="mask_bias",
+    )(mask)
+
+
+def attend_rows(bias_ref, src_ref, rows, gain_ref, tile_refs):
     count = rows.stop - rows.start
     channels = src_ref.shape[1]
-    tile_rows = tile_refs[0].shape[1]
-    keys = len(tile_refs) * tile_rows
-    heads = LANES // count
-    width = heads * HD
-    sign = 1 - 2 * (lax.axis_index("tile") % 2)
+    width = LANES // count * HD
     x = src_ref[rows, :].astype(jnp.float32)
     inv = lax.rsqrt(jnp.mean(x * x, axis=-1, keepdims=True) + 1e-06)
-    key = lax.broadcasted_iota(jnp.int32, (keys, LANES), 0)
-    bias = jnp.full((keys, LANES), NEG, jnp.float32)
-    for s, offset in enumerate(SLOTS):
-        bit = mask_ref[0, WIN + sign * offset]
-        here = (key >= s * tile_rows) & (key < (s + 1) * tile_rows) & (bit > 0)
-        bias = jnp.where(here, 0.0, bias)
     zero = jnp.zeros((count, HD), jnp.bfloat16)
-    groups = [slice(c, c + width) for c in range(0, channels, width)]
+    groups = [slice(c, min(c + width, channels)) for c in range(0, channels, width)]
+    sizes = [(g.stop - g.start) // HD for g in groups]
     states = [src_ref[rows, g].astype(jnp.float32) for g in groups]
     queries = []
-    for g, state in zip(groups, states):
+    for g, heads, state in zip(groups, sizes, states):
         query = (state * inv * gain_ref[:, g]).astype(jnp.bfloat16)
         blocks = [
             jnp.concatenate(
@@ -88,8 +98,8 @@
             (((1,), (1,)), ((), ())),
             preferred_element_type=jnp.float32,
         )
-        + bias
-        for g, query in zip(groups, queries)
+        + bias_ref[:, : heads * count]
+        for g, heads, query in zip(groups, sizes, queries)
     ]
     tops = [jnp.max(s, axis=0, keepdims=True) for s in scores]
     weights = [jnp.exp2((s - top) * (HD**-0.5 * LOG2E)) for s, top in zip(scores, tops)]
@@ -104,8 +114,8 @@
         for g, w in zip(groups, weights)
     ]
     done = []
-    for g, state, m, total in zip(groups, states, mixed, totals):
-        by_row = jnp.transpose(jnp.broadcast_to(total, (LANES, LANES)))
+    for g, heads, state, m, total in zip(groups, sizes, states, mixed, totals):
+        by_row = jnp.transpose(jnp.broadcast_to(total, (HD, heads * count)))
         result = jnp.concatenate(
             [
                 m[b * count : (b + 1) * count, b * HD : (b + 1) * HD]
@@ -118,18 +128,24 @@
     return done
 
 
-def attend_body(moment, has_next, rows, mask_ref, src_ref, gain_ref, *refs):
+def attend_body(moment, has_next, rows, joined, bias_ref, src_ref, gain_ref, *refs):
     tile_refs = refs[: len(SLOTS)]
     rest = list(refs[len(SLOTS) :])
     kept_ref = rest.pop(0) if moment else None
+    earlier_refs = [rest.pop(0) for _ in range(joined)]
     out_ref = rest.pop(0)
     next_ref = rest.pop(0) if has_next else None
     live = lax.axis_index("section") == moment
+    at = 0
+    for ref in earlier_refs:
+        out_ref[at : at + ref.shape[0], :] = ref[...]
+        at += ref.shape[0]
+    span = slice(at, at + rows.stop - rows.start)
 
     @pl.when(live)
     def _():
-        for g, state, result in attend_rows(mask_ref, src_ref, rows, gain_ref, tile_refs):
-            out_ref[:, g] = result
+        for g, state, result in attend_rows(bias_ref, src_ref, rows, gain_ref, tile_refs):
+            out_ref[span, g] = result
             if has_next:
                 next_ref[:, g] = (state + result.astype(jnp.float32)).astype(jnp.bfloat16)
 
@@ -137,21 +153,23 @@
 
         @pl.when(jnp.logical_not(live))
         def _():
-            out_ref[...] = kept_ref[...]
-
-
-def attend(moment, has_next, rows, mask, source, gain, tiles, kept):
+            out_ref[span, :] = kept_ref[...]
+
+
+def attend(moment, has_next, rows, bias, source, gain, tiles, kept, earlier=()):
     count = rows.stop - rows.start
     channels = source.shape[1]
-    shape = jax.ShapeDtypeStruct((count, channels), jnp.bfloat16)
     keys = len(tiles) * tiles[0].shape[1]
-    operands = [mask, source, gain, *tiles] + ([kept] if moment else [])
-    outputs = 2 if has_next else 1
+    operands = [bias, source, gain, *tiles] + ([kept] if moment else []) + list(earlier)
+    total = count + sum(e.shape[0] for e in earlier)
+    shapes = [jax.ShapeDtypeStruct((total, channels), jnp.bfloat16)]
+    if has_next:
+        shapes.append(jax.ShapeDtypeStruct((count, channels), jnp.bfloat16))
     return pl.pallas_call(
-        functools.partial(attend_body, moment, has_next, rows),
-        out_shape=(shape,) * outputs,
-        in_specs=[smem()] + [vmem()] * (len(operands) - 1),
-        out_specs=(vmem(),) * outputs,
+        functools.partial(attend_body, moment, has_next, rows, len(earlier)),
+        out_shape=tuple(shapes),
+        in_specs=[vmem()] * len(operands),
+        out_specs=(vmem(),) * len(shapes),
         compiler_params=pltpu.CompilerParams(vmem_limit_bytes=ATTEND_VMEM),
         cost_estimate=pl.CostEstimate(
             flops=4 * count * keys * channels,
@@ -189,19 +207,22 @@
     rows = hidden.shape[0]
     count = rows // PIECES
     own = split_keys_values(keys_values[0])
+    bias = mask_bias(tile_mask, rows)
     window = exchange(own, lax.axis_size("tile"))
     sources = [(hidden, slice(p * count, (p + 1) * count)) for p in range(PIECES)]
     kept = [None] * PIECES
     for moment in range(sections):
         has_next = moment + 1 < sections
         for p, (source, span) in enumerate(sources):
-            results = attend(moment, has_next, span, tile_mask, source, q_gain, window, kept[p])
+            earlier = kept[:p] if not has_next and p + 1 == PIECES else ()
+            results = attend(
+                moment, has_next, span, bias, source, q_gain, window, kept[p], earlier
+            )
             kept[p] = results[0]
             if has_next:
                 arrived = lax.ppermute(results[1], "section", [(moment, moment + 1)])
                 sources[p] = (arrived, slice(0, count))
-    attended = kept[0] if PIECES == 1 else jnp.concatenate(kept, axis=0)
-    return attended[None]
+    return kept[-1][None]
 
 
 def solution(mesh):

time: 63.4 us -> 61.9 us (0.976)
  the two profiles are of different devices: /device:TPU:14 before, /device:TPU:22 now
where the time goes in v1:
time: 61.9 us; the launch traced here: 61.6 us
  waiting for transfers between devices  41.8 us (68%)
  starting transfers between devices  13.9 us (22%)
  Pallas kernels  4.57 us (7%)
  local copies, waits for them, and re-layouts  1.1 us (2%)
    ppermute x6, waiting for transfers between devices, move(): return lax.ppermute(tile, 'tile', pairs)  21.9 us
    ppermute x6, waiting for transfers between devices, on_device(): arrived = lax.ppermute(results[1], 'section', [(moment, moment + 1)])  19.9 us
    ppermute x6, starting transfers between devices, move(): return lax.ppermute(tile, 'tile', pairs)  8.64 us
    ppermute x6, starting transfers between devices, on_device(): arrived = lax.ppermute(results[1], 'section', [(moment, moment + 1)])  5.26 us
    pallas_call x8, Pallas kernels, attend(): pl.pallas_call(functools.partial(attend_body, moment, has_next, rows, len...  3.55 us
  transfers between devices with their start and end apart: 12, of which 4 were waited for; matrix products, arithmetic and copies ran while one was open for 0% of the time, Pallas kernels for 3%

profile of v1, /device:TPU:22, one launch (start us, length us, event | category | flops | bytes accessed | tf_op | source)
XLA Modules:
  0.0 61.6 jit_solution(2979427629885392386)
XLA Ops:
  0.0 0.0 copy-start.2
  0.0 1.1 %copy-done.2 = bf16[1,64,2,2560]{3,2,1,0:T(2,128)(2,1)S(1)} copy-done((bf16[1,64,2,2560]{3,2,1,0:T(2,128)(2,1)S(1)}, bf16[1,64,2,2560]{3,2,1,0:T(2,128)(2,1)}, u32[]{:S(2)}) %copy-start.2) | copy-done | bytes 655384
  1.1 0.0 copy-start.3
  1.1 0.0 copy-start
  1.1 0.4 split_kv.1.refs_0_
  1.5 0.0 copy-start.1
  1.5 3.5 %collective-permute-start.1 = (bf16[2,64,2560]{2,1,0:T(8,128)(2,1)S(1)}, bf16[2,64,2560]{2,1,0:T(8,128)(2,1)S(1)}, u32[]{:S(2)}, u32[]{:S(2)}) collective-permute-start(bf16[2,64,2560]{2,1,0:T(8,128)(2,1)S(1)} %split_kv.1.refs_0_), channel_id=1, source_target_pairs={{3,1},{5,3},{7,5},{0,2},{2,4},{4,6},{11,9},{13,11},{15,13},{8,10},... | collective-permute-start | bytes 1966088 | tf_op jit(solution)/shard_map/ppermute | solution.py:191
  5.0 2.4 %collective-permute-start = (bf16[2,64,2560]{2,1,0:T(8,128)(2,1)S(1)}, bf16[2,64,2560]{2,1,0:T(8,128)(2,1)S(1)}, u32[]{:S(2)}, u32[]{:S(2)}) collective-permute-start(bf16[2,64,2560]{2,1,0:T(8,128)(2,1)S(1)} %split_kv.1.refs_0_), channel_id=1, source_target_pairs={{1,3},{3,5},{5,7},{2,0},{4,2},{6,4},{9,11},{11,13},{13,15},{10,8},... | collective-permute-start | bytes 1966088 | tf_op jit(solution)/shard_map/ppermute | solution.py:191
  7.4 0.1 collective-permute-start.3
  7.5 12.6 %collective-permute-done.1.refs_2_ = bf16[2,64,2560]{2,1,0:T(8,128)(2,1)S(1)} collective-permute-done((bf16[2,64,2560]{2,1,0:T(8,128)(2,1)S(1)}, bf16[2,64,2560]{2,1,0:T(8,128)(2,1)S(1)}, u32[]{:S(2)}, u32[]{:S(2)}) %collective-permute-start.1) | collective-permute-done | bytes 655392 | tf_op jit(solution)/shard_map/ppermute | solution.py:191
  20.1 0.0 collective-permute-start.5
  20.1 0.0 collective-permute-done.refs_1_
  20.1 0.8 %collective-permute-start.4 = (bf16[2,64,2560]{2,1,0:T(8,128)(2,1)S(1)}, bf16[2,64,2560]{2,1,0:T(8,128)(2,1)S(1)}, u32[]{:S(2)}, u32[]{:S(2)}) collective-permute-start(bf16[2,64,2560]{2,1,0:T(8,128)(2,1)S(1)} %collective-permute-done.refs_1_), channel_id=1, source_target_pairs={{0,1},{1,0},{2,3},{3,2},{4,5},{5,4},{6,7},{7,6},{8,9},{9,8},{10,11... | collective-permute-start | bytes 1966088 | tf_op jit(solution)/shard_map/ppermute | solution.py:191
  20.9 2.0 %collective-permute-start.2 = (bf16[2,64,2560]{2,1,0:T(8,128)(2,1)S(1)}, bf16[2,64,2560]{2,1,0:T(8,128)(2,1)S(1)}, u32[]{:S(2)}, u32[]{:S(2)}) collective-permute-start(bf16[2,64,2560]{2,1,0:T(8,128)(2,1)S(1)} %collective-permute-done.refs_1_), channel_id=1, source_target_pairs={{1,2},{3,4},{5,6},{2,1},{4,3},{6,5},{9,10},{11,12},{13,14},{10,9},... | collective-permute-start | bytes 1966088 | tf_op jit(solution)/shard_map/ppermute | solution.py:191
  22.8 0.0 copy-done.3
  22.8 0.6 mask_bias.1.bias_ref
  23.4 0.0 collective-permute-done.3.refs_4_
  23.4 0.0 collective-permute-done.5.refs_6_
  23.4 0.0 collective-permute-done.4.refs_5_
  23.5 9.3 %collective-permute-done.2.refs_3_ = bf16[2,64,2560]{2,1,0:T(8,128)(2,1)S(1)} collective-permute-done((bf16[2,64,2560]{2,1,0:T(8,128)(2,1)S(1)}, bf16[2,64,2560]{2,1,0:T(8,128)(2,1)S(1)}, u32[]{:S(2)}, u32[]{:S(2)}) %collective-permute-start.2) | collective-permute-done | bytes 655392 | tf_op jit(solution)/shard_map/ppermute | solution.py:191
  32.8 0.0 copy-done
  32.8 0.0 copy-done.1
  32.8 0.7 %collective-permute-start.9 = (bf16[32,2560]{1,0:T(8,128)(2,1)S(1)}, bf16[32,2560]{1,0:T(8,128)(2,1)S(1)}, u32[]{:S(2)}, u32[]{:S(2)}) collective-permute-start(bf16[32,2560]{1,0:T(8,128)(2,1)S(1)} %get-tuple-element.23), channel_id=1, source_target_pairs={{0,8},{1,9},{2,10},{3,11},{4,12},{5,13},{6,14},{7,15}} | collective-permute-start | bytes 491528 | tf_op jit(solution)/shard_map/ppermute | solution.py:223
  33.5 0.7 %collective-permute-start.6 = (bf16[32,2560]{1,0:T(8,128)(2,1)S(1)}, bf16[32,2560]{1,0:T(8,128)(2,1)S(1)}, u32[]{:S(2)}, u32[]{:S(2)}) collective-permute-start(bf16[32,2560]{1,0:T(8,128)(2,1)S(1)} %get-tuple-element.17), channel_id=1, source_target_pairs={{0,8},{1,9},{2,10},{3,11},{4,12},{5,13},{6,14},{7,15}} | collective-permute-start | bytes 491528 | tf_op jit(solution)/shard_map/ppermute | solution.py:223
  34.1 0.0 collective-permute-done.9.src_ref
  34.2 0.7 %collective-permute-start.10 = (bf16[32,2560]{1,0:T(8,128)(2,1)S(1)}, bf16[32,2560]{1,0:T(8,128)(2,1)S(1)}, u32[]{:S(2)}, u32[]{:S(2)}) collective-permute-start(bf16[32,2560]{1,0:T(8,128)(2,1)S(1)} %get-tuple-element.25), channel_id=1, source_target_pairs={{8,16},{9,17},{10,18},{11,19},{12,20},{13,21},{14,22},{15,23}} | collective-permute-start | bytes 491528 | tf_op jit(solution)/shard_map/ppermute | solution.py:223
  34.9 0.0 collective-permute-done.6.src_ref
  34.9 0.7 %collective-permute-start.7 = (bf16[32,2560]{1,0:T(8,128)(2,1)S(1)}, bf16[32,2560]{1,0:T(8,128)(2,1)S(1)}, u32[]{:S(2)}, u32[]{:S(2)}) collective-permute-start(bf16[32,2560]{1,0:T(8,128)(2,1)S(1)} %get-tuple-element.19), channel_id=1, source_target_pairs={{8,16},{9,17},{10,18},{11,19},{12,20},{13,21},{14,22},{15,23}} | collective-permute-start | bytes 491528 | tf_op jit(solution)/shard_map/ppermute | solution.py:223
  35.6 0.0 collective-permute-done.10.src_ref
  35.6 1.3 %collective-permute-start.11 = (bf16[32,2560]{1,0:T(8,128)(2,1)S(1)}, bf16[32,2560]{1,0:T(8,128)(2,1)S(1)}, u32[]{:S(2)}, u32[]{:S(2)}) collective-permute-start(bf16[32,2560]{1,0:T(8,128)(2,1)S(1)} %get-tuple-element.27), channel_id=1, source_target_pairs={{16,24},{17,25},{18,26},{19,27},{20,28},{21,29},{22,30},{23,31}} | collective-permute-start | bytes 491528 | tf_op jit(solution)/shard_map/ppermute | solution.py:223
  37.0 0.0 collective-permute-done.7.src_ref
  37.0 1.3 %collective-permute-start.8 = (bf16[32,2560]{1,0:T(8,128)(2,1)S(1)}, bf16[32,2560]{1,0:T(8,128)(2,1)S(1)}, u32[]{:S(2)}, u32[]{:S(2)}) collective-permute-start(bf16[32,2560]{1,0:T(8,128)(2,1)S(1)} %get-tuple-element.21), channel_id=1, source_target_pairs={{16,24},{17,25},{18,26},{19,27},{20,28},{21,29},{22,30},{23,31}} | collective-permute-start | bytes 491528 | tf_op jit(solution)/shard_map/ppermute | solution.py:223
  38.3 18.0 %collective-permute-done.11.src_ref = bf16[32,2560]{1,0:T(8,128)(2,1)S(1)} collective-permute-done((bf16[32,2560]{1,0:T(8,128)(2,1)S(1)}, bf16[32,2560]{1,0:T(8,128)(2,1)S(1)}, u32[]{:S(2)}, u32[]{:S(2)}) %collective-permute-start.11) | collective-permute-done | bytes 163872 | tf_op jit(solution)/shard_map/ppermute | solution.py:223
  56.3 1.3 %attend.14.refs_8_ = bf16[32,2560]{1,0:T(8,128)(2,1)S(1)} custom-call(f32[448,128]{1,0:T(8,128)S(1)} %mask_bias.1.bias_ref, bf16[32,2560]{1,0:T(8,128)(2,1)S(1)} %collective-permute-done.11.src_ref, f32[1,2560]{1,0:T(1,128)S(1)} %copy-done.1, bf16[2,64,2560]{2,1,0:T(8,128)(2,1)S(1)} %split_kv.1.refs_0_, ...), custom_call_target="tpu_custom_call" | custom-call | flops 146800640 | bytes 5079040 | tf_op jit(solution)/shard_map/attend/pallas_call | solution.py:168
  57.6 1.9 %collective-permute-done.8.src_ref = bf16[32,2560]{1,0:T(8,128)(2,1)S(1)} collective-permute-done((bf16[32,2560]{1,0:T(8,128)(2,1)S(1)}, bf16[32,2560]{1,0:T(8,128)(2,1)S(1)}, u32[]{:S(2)}, u32[]{:S(2)}) %collective-permute-start.8) | collective-permute-done | bytes 163872 | tf_op jit(solution)/shard_map/ppermute | solution.py:223
  59.6 2.1 %attend.15 = bf16[64,2560]{1,0:T(8,128)(2,1)} custom-call(f32[448,128]{1,0:T(8,128)S(1)} %mask_bias.1.bias_ref, bf16[32,2560]{1,0:T(8,128)(2,1)S(1)} %collective-permute-done.8.src_ref, f32[1,2560]{1,0:T(1,128)S(1)} %copy-done.1, bf16[2,64,2560]{2,1,0:T(8,128)(2,1)S(1)} %split_kv.1.refs_0_, bf16[2,64,2560]{2,1,0:T(8,128)(2,1)S(1)} %collective-permute-done.refs_1_, ...), custom_call_target="tpu_custom_call" | custom-call | flops 146800640 | bytes 5079040 | tf_op jit(solution)/shard_map/attend/pallas_call | solution.py:168
  (6 shorter events, 0.1 us)
Async XLA Ops:
  0.0 1.1 %copy-start.2 = (bf16[1,64,2,2560]{3,2,1,0:T(2,128)(2,1)S(1)}, bf16[1,64,2,2560]{3,2,1,0:T(2,128)(2,1)}, u32[]{:S(2)}) copy-start(bf16[1,64,2,2560]{3,2,1,0:T(2,128)(2,1)} %param.5) | copy-start | bytes 1966084
  1.1 21.7 %copy-start.3 = (s32[1,7]{1,0:T(1,128)S(1)}, s32[1,7]{1,0:T(1,128)}, u32[]{:S(2)}) copy-start(s32[1,7]{1,0:T(1,128)} %mask_ref.1) | copy-start | bytes 88
  1.1 31.7 %copy-start = (bf16[64,2560]{1,0:T(8,128)(2,1)S(1)}, bf16[64,2560]{1,0:T(8,128)(2,1)}, u32[]{:S(2)}) copy-start(bf16[64,2560]{1,0:T(8,128)(2,1)} %src_ref.3) | copy-start | bytes 983044
  1.5 31.2 %copy-start.1 = (f32[1,2560]{1,0:T(1,128)S(1)}, f32[1,2560]{1,0:T(1,128)}, u32[]{:S(2)}) copy-start(f32[1,2560]{1,0:T(1,128)} %gain_ref.15) | copy-start | bytes 30724
  1.5 18.5 %collective-permute-start.1 = (bf16[2,64,2560]{2,1,0:T(8,128)(2,1)S(1)}, bf16[2,64,2560]{2,1,0:T(8,128)(2,1)S(1)}, u32[]{:S(2)}, u32[]{:S(2)}) collective-permute-start(bf16[2,64,2560]{2,1,0:T(8,128)(2,1)S(1)} %split_kv.1.refs_0_), channel_id=1, source_target_pairs={{3,1},{5,3},{7,5},{0,2},{2,4},{4,6},{11,9},{13,11},{15,13},{8,10},... | collective-permute-start | bytes 1966088 | tf_op jit(solution)/shard_map/ppermute | solution.py:191
  5.0 15.1 %collective-permute-start = (bf16[2,64,2560]{2,1,0:T(8,128)(2,1)S(1)}, bf16[2,64,2560]{2,1,0:T(8,128)(2,1)S(1)}, u32[]{:S(2)}, u32[]{:S(2)}) collective-permute-start(bf16[2,64,2560]{2,1,0:T(8,128)(2,1)S(1)} %split_kv.1.refs_0_), channel_id=1, source_target_pairs={{1,3},{3,5},{5,7},{2,0},{4,2},{6,4},{9,11},{11,13},{13,15},{10,8},... | collective-permute-start | bytes 1966088 | tf_op jit(solution)/shard_map/ppermute | solution.py:191
  7.4 16.0 %collective-permute-start.3 = (bf16[2,64,2560]{2,1,0:T(8,128)(2,1)S(1)}, bf16[2,64,2560]{2,1,0:T(8,128)(2,1)S(1)}, u32[]{:S(2)}, u32[]{:S(2)}) collective-permute-start(bf16[2,64,2560]{2,1,0:T(8,128)(2,1)S(1)} %split_kv.1.refs_0_), channel_id=1, source_target_pairs={{0,1},{1,0},{2,3},{3,2},{4,5},{5,4},{6,7},{7,6},{8,9},{9,8},{10,11... | collective-permute-start | bytes 1966088 | tf_op jit(solution)/shard_map/ppermute | solution.py:191
  20.1 3.3 %collective-permute-start.5 = (bf16[2,64,2560]{2,1,0:T(8,128)(2,1)S(1)}, bf16[2,64,2560]{2,1,0:T(8,128)(2,1)S(1)}, u32[]{:S(2)}, u32[]{:S(2)}) collective-permute-start(bf16[2,64,2560]{2,1,0:T(8,128)(2,1)S(1)} %collective-permute-done.1.refs_2_), channel_id=1, source_target_pairs={{0,1},{1,0},{2,3},{3,2},{4,5},{5,4},{6,7},{7,6},{8,9},{9,8},{10,11... | collective-permute-start | bytes 1966088 | tf_op jit(solution)/shard_map/ppermute | solution.py:191
  20.1 3.3 %collective-permute-start.4 = (bf16[2,64,2560]{2,1,0:T(8,128)(2,1)S(1)}, bf16[2,64,2560]{2,1,0:T(8,128)(2,1)S(1)}, u32[]{:S(2)}, u32[]{:S(2)}) collective-permute-start(bf16[2,64,2560]{2,1,0:T(8,128)(2,1)S(1)} %collective-permute-done.refs_1_), channel_id=1, source_target_pairs={{0,1},{1,0},{2,3},{3,2},{4,5},{5,4},{6,7},{7,6},{8,9},{9,8},{10,11... | collective-permute-start | bytes 1966088 | tf_op jit(solution)/shard_map/ppermute | solution.py:191
  20.9 11.9 %collective-permute-start.2 = (bf16[2,64,2560]{2,1,0:T(8,128)(2,1)S(1)}, bf16[2,64,2560]{2,1,0:T(8,128)(2,1)S(1)}, u32[]{:S(2)}, u32[]{:S(2)}) collective-permute-start(bf16[2,64,2560]{2,1,0:T(8,128)(2,1)S(1)} %collective-permute-done.refs_1_), channel_id=1, source_target_pairs={{1,2},{3,4},{5,6},{2,1},{4,3},{6,5},{9,10},{11,12},{13,14},{10,9},... | collective-permute-start | bytes 1966088 | tf_op jit(solution)/shard_map/ppermute | solution.py:191
  32.8 1.4 %collective-permute-start.9 = (bf16[32,2560]{1,0:T(8,128)(2,1)S(1)}, bf16[32,2560]{1,0:T(8,128)(2,1)S(1)}, u32[]{:S(2)}, u32[]{:S(2)}) collective-permute-start(bf16[32,2560]{1,0:T(8,128)(2,1)S(1)} %get-tuple-element.23), channel_id=1, source_target_pairs={{0,8},{1,9},{2,10},{3,11},{4,12},{5,13},{6,14},{7,15}} | collective-permute-start | bytes 491528 | tf_op jit(solution)/shard_map/ppermute | solution.py:223
  33.5 1.4 %collective-permute-start.6 = (bf16[32,2560]{1,0:T(8,128)(2,1)S(1)}, bf16[32,2560]{1,0:T(8,128)(2,1)S(1)}, u32[]{:S(2)}, u32[]{:S(2)}) collective-permute-start(bf16[32,2560]{1,0:T(8,128)(2,1)S(1)} %get-tuple-element.17), channel_id=1, source_target_pairs={{0,8},{1,9},{2,10},{3,11},{4,12},{5,13},{6,14},{7,15}} | collective-permute-start | bytes 491528 | tf_op jit(solution)/shard_map/ppermute | solution.py:223
  34.2 1.4 %collective-permute-start.10 = (bf16[32,2560]{1,0:T(8,128)(2,1)S(1)}, bf16[32,2560]{1,0:T(8,128)(2,1)S(1)}, u32[]{:S(2)}, u32[]{:S(2)}) collective-permute-start(bf16[32,2560]{1,0:T(8,128)(2,1)S(1)} %get-tuple-element.25), channel_id=1, source_target_pairs={{8,16},{9,17},{10,18},{11,19},{12,20},{13,21},{14,22},{15,23}} | collective-permute-start | bytes 491528 | tf_op jit(solution)/shard_map/ppermute | solution.py:223
  34.9 2.0 %collective-permute-start.7 = (bf16[32,2560]{1,0:T(8,128)(2,1)S(1)}, bf16[32,2560]{1,0:T(8,128)(2,1)S(1)}, u32[]{:S(2)}, u32[]{:S(2)}) collective-permute-start(bf16[32,2560]{1,0:T(8,128)(2,1)S(1)} %get-tuple-element.19), channel_id=1, source_target_pairs={{8,16},{9,17},{10,18},{11,19},{12,20},{13,21},{14,22},{15,23}} | collective-permute-start | bytes 491528 | tf_op jit(solution)/shard_map/ppermute | solution.py:223
  35.6 20.6 %collective-permute-start.11 = (bf16[32,2560]{1,0:T(8,128)(2,1)S(1)}, bf16[32,2560]{1,0:T(8,128)(2,1)S(1)}, u32[]{:S(2)}, u32[]{:S(2)}) collective-permute-start(bf16[32,2560]{1,0:T(8,128)(2,1)S(1)} %get-tuple-element.27), channel_id=1, source_target_pairs={{16,24},{17,25},{18,26},{19,27},{20,28},{21,29},{22,30},{23,31}} | collective-permute-start | bytes 491528 | tf_op jit(solution)/shard_map/ppermute | solution.py:223
  37.0 22.6 %collective-permute-start.8 = (bf16[32,2560]{1,0:T(8,128)(2,1)S(1)}, bf16[32,2560]{1,0:T(8,128)(2,1)S(1)}, u32[]{:S(2)}, u32[]{:S(2)}) collective-permute-start(bf16[32,2560]{1,0:T(8,128)(2,1)S(1)} %get-tuple-element.21), channel_id=1, source_target_pairs={{16,24},{17,25},{18,26},{19,27},{20,28},{21,29},{22,30},{23,31}} | collective-permute-start | bytes 491528 | tf_op jit(solution)/shard_map/ppermute | solution.py:223

commit v2 on v1

v2 whole, which is shorter than its diff:
```python
import functools

import jax
import jax.numpy as jnp
from jax import lax
from jax.experimental import pallas as pl
from jax.experimental.pallas import tpu as pltpu
from jax.sharding import PartitionSpec as P


HD = 128
WIN = 3
LANES = 128
NEG = -1e30
SCALE = HD**-0.5 * 1.4426950408889634
PIECES = 2
SLOTS = (0, 2, -2, -3, 1, -1, 3)
ATTEND_VMEM = 24 << 20
SPLIT_VMEM = 8 << 20


def vmem():
    return pl.BlockSpec(memory_space=pltpu.VMEM)


def smem():
    return pl.BlockSpec(memory_space=pltpu.SMEM)


def split_body(kv_ref, out_ref):
    rows = kv_ref.shape[0]
    i = lax.broadcasted_iota(jnp.int32, (2 * rows, 2 * rows), 0)
    j = lax.broadcasted_iota(jnp.int32, (2 * rows, 2 * rows), 1)
    source = jnp.where(i < rows, 2 * i, 2 * (i - rows) + 1)
    sort = jnp.where(j == source, 1.0, 0.0).astype(jnp.bfloat16)
    for c in range(0, kv_ref.shape[2], HD):
        mixed = kv_ref[:, :, c : c + HD].reshape(2 * rows, HD)
        both = jnp.dot(sort, mixed, preferred_element_type=jnp.float32).astype(jnp.bfloat16)
        out_ref[0, :, c : c + HD] = both[:rows]
        out_ref[1, :, c : c + HD] = both[rows:]


def split_keys_values(kv):
    rows, _, channels = kv.shape
    return pl.pallas_call(
        split_body,
        out_shape=jax.ShapeDtypeStruct((2, rows, channels), jnp.bfloat16),
        in_specs=[vmem()],
        out_specs=vmem(),
        compiler_params=pltpu.CompilerParams(vmem_limit_bytes=SPLIT_VMEM),
        name="split_kv",
    )(kv)


def bias_body(tile_rows, mask_ref, out_ref):
    sign = 1 - 2 * (lax.axis_index("tile") % 2)
    for s, offset in enumerate(SLOTS):
        bit = mask_ref[0, WIN + sign * offset]
        block = jnp.full((tile_rows, LANES), jnp.where(bit > 0, 0.0, NEG), jnp.float32)
        out_ref[s * tile_rows : (s + 1) * tile_rows, :] = block


def mask_bias(mask, tile_rows):
    return pl.pallas_call(
        functools.partial(bias_body, tile_rows),
        out_shape=jax.ShapeDtypeStruct((len(SLOTS) * tile_rows, LANES), jnp.float32),
        in_specs=[smem()],
        out_specs=vmem(),
        compiler_params=pltpu.CompilerParams(vmem_limit_bytes=SPLIT_VMEM),
        name="mask_bias",
    )(mask)


def head_groups(count, channels):
    width = LANES // count * HD
    groups = [slice(c, min(c + width, channels)) for c in range(0, channels, width)]
    return groups, [(g.stop - g.start) // HD for g in groups]


def per_row(lanes, heads, count):
    return jnp.transpose(jnp.broadcast_to(lanes, (HD, heads * count)))


def attend_tiles(bias, src_ref, rows, gain_ref, tile_refs):
    count = rows.stop - rows.start
    groups, sizes = head_groups(count, src_ref.shape[1])
    x = src_ref[rows, :].astype(jnp.float32)
    inv = lax.rsqrt(jnp.mean(x * x, axis=-1, keepdims=True) + 1e-06)
    zero = jnp.zeros((count, HD), jnp.bfloat16)
    states = [src_ref[rows, g].astype(jnp.float32) for g in groups]
    queries = []
    for g, heads, state in zip(groups, sizes, states):
        query = (state * inv * gain_ref[:, g]).astype(jnp.bfloat16)
        blocks = [
            jnp.concatenate(
                [query[:, b * HD : (b + 1) * HD] if a == b else zero for b in range(heads)], axis=1
            )
            for a in range(heads)
        ]
        queries.append(jnp.concatenate(blocks, axis=0))
    scores = [
        lax.dot_general(
            jnp.concatenate([t[0, :, g] for t in tile_refs], axis=0),
            query,
            (((1,), (1,)), ((), ())),
            preferred_element_type=jnp.float32,
        )
        + bias[:, : heads * count]
        for g, heads, query in zip(groups, sizes, queries)
    ]
    tops = [jnp.max(s, axis=0, keepdims=True) for s in scores]

    def weigh(tops):
        weights = [jnp.exp2((s - top) * SCALE) for s, top in zip(scores, tops)]
        totals = [jnp.sum(w, axis=0, keepdims=True) for w in weights]
        mixed = [
            lax.dot_general(
                w.astype(jnp.bfloat16),
                jnp.concatenate([t[1, :, g] for t in tile_refs], axis=0),
                (((0,), (0,)), ((), ())),
                preferred_element_type=jnp.float32,
            )
            for g, w in zip(groups, weights)
        ]
        blocks = [
            [m[b * count : (b + 1) * count, b * HD : (b + 1) * HD] for b in range(heads)]
            for m, heads in zip(mixed, sizes)
        ]
        return totals, blocks

    return states, tops, weigh


def attend_rows(bias_ref, src_ref, rows, gain_ref, tile_refs):
    count = rows.stop - rows.start
    groups, sizes = head_groups(count, src_ref.shape[1])
    states, tops, weigh = attend_tiles(bias_ref[...], src_ref, rows, gain_ref, tile_refs)
    totals, mixed = weigh(tops)
    done = []
    for g, heads, state, blocks, total in zip(groups, sizes, states, mixed, totals):
        by_row = per_row(total, heads, count)
        parts = [m / by_row[b * count : (b + 1) * count] for b, m in enumerate(blocks)]
        done.append((g, state, jnp.concatenate(parts, axis=1).astype(jnp.bfloat16)))
    return done


def partial_body(slots, carried, last, bias_ref, src_ref, gain_ref, *refs):
    tile_refs = refs[: len(slots)]
    refs = refs[len(slots) :]
    top_in, total_in, sum_in = refs[:3] if carried else (None,) * 3
    refs = refs[3:] if carried else refs
    rows, channels = src_ref.shape
    tile_rows = tile_refs[0].shape[1]
    groups, sizes = head_groups(rows, channels)

    @pl.when(lax.axis_index("section") == 0)
    def _():
        bias = jnp.concatenate(
            [bias_ref[s * tile_rows : (s + 1) * tile_rows, :] for s in slots], axis=0
        )
        states, tops, weigh = attend_tiles(bias, src_ref, slice(0, rows), gain_ref, tile_refs)
        if carried:
            tops = [jnp.maximum(t, top_in[n : n + 1, :]) for n, t in enumerate(tops)]
        totals, sums = weigh(tops)
        for n, (g, heads) in enumerate(zip(groups, sizes)):
            total, blocks = totals[n], sums[n]
            if carried:
                fade = jnp.exp2((top_in[n : n + 1, :] - tops[n]) * SCALE)
                total = total + fade * total_in[n : n + 1, :]
                by_row = per_row(fade, heads, rows)
                blocks = [
                    m
                    + by_row[b * rows : (b + 1) * rows]
                    * sum_in[:, g.start + b * HD : g.start + (b + 1) * HD]
                    for b, m in enumerate(blocks)
                ]
            if not last:
                top_out, total_out, sum_out = refs
                top_out[n : n + 1, :] = tops[n]
                total_out[n : n + 1, :] = total
                for b, m in enumerate(blocks):
                    sum_out[:, g.start + b * HD : g.start + (b + 1) * HD] = m
                continue
            by_row = per_row(total, heads, rows)
            parts = [m / by_row[b * rows : (b + 1) * rows] for b, m in enumerate(blocks)]
            result = jnp.concatenate(parts, axis=1).astype(jnp.bfloat16)
            state = (states[n] + result.astype(jnp.float32)).astype(jnp.bfloat16)
            count = rows // PIECES
            for p in range(PIECES):
                span = slice(p * count, (p + 1) * count)
                refs[p][:, g] = result[span]
                refs[PIECES + p][:, g] = state[span]


def partial_attend(slots, last, bias, source, gain, tiles, carry=()):
    rows, channels = source.shape
    if last:
        piece = jax.ShapeDtypeStruct((rows // PIECES, channels), jnp.bfloat16)
        shapes = (piece,) * (2 * PIECES)
    else:
        lanes = jax.ShapeDtypeStruct((len(head_groups(rows, channels)[0]), LANES), jnp.float32)
        shapes = (lanes, lanes, jax.ShapeDtypeStruct((rows, channels), jnp.float32))
    operands = [bias, source, gain, *tiles, *carry]
    keys = len(tiles) * rows
    return pl.pallas_call(
        functools.partial(partial_body, slots, bool(carry), last),
        out_shape=shapes,
        in_specs=[vmem()] * len(operands),
        out_specs=(vmem(),) * len(shapes),
        compiler_params=pltpu.CompilerParams(vmem_limit_bytes=ATTEND_VMEM),
        cost_estimate=pl.CostEstimate(
            flops=4 * rows * keys * channels,
            bytes_accessed=4 * keys * channels + 6 * rows * channels,
            transcendentals=rows * keys * channels // HD,
        ),
        name="partial_attend",
    )(*operands)


def attend_body(moment, has_next, joined, bias_ref, src_ref, gain_ref, *refs):
    tile_refs = refs[: len(SLOTS)]
    rest = list(refs[len(SLOTS) :])
    kept_ref = rest.pop(0)
    earlier_refs = [rest.pop(0) for _ in range(joined)]
    out_ref = rest.pop(0)
    next_ref = rest.pop(0) if has_next else None
    live = lax.axis_index("section") == moment
    at = 0
    for ref in earlier_refs:
        out_ref[at : at + ref.shape[0], :] = ref[...]
        at += ref.shape[0]
    rows = src_ref.shape[0]
    span = slice(at, at + rows)

    @pl.when(live)
    def _():
        for g, state, result in attend_rows(bias_ref, src_ref, slice(0, rows), gain_ref, tile_refs):
            out_ref[span, g] = result
            if has_next:
                next_ref[:, g] = (state + result.astype(jnp.float32)).astype(jnp.bfloat16)

    @pl.when(jnp.logical_not(live))
    def _():
        out_ref[span, :] = kept_ref[...]


def attend(moment, has_next, bias, source, gain, tiles, kept, earlier):
    count, channels = source.shape
    keys = len(tiles) * tiles[0].shape[1]
    operands = [bias, source, gain, *tiles, kept, *earlier]
    total = count + sum(e.shape[0] for e in earlier)
    shapes = [jax.ShapeDtypeStruct((total, channels), jnp.bfloat16)]
    if has_next:
        shapes.append(jax.ShapeDtypeStruct((count, channels), jnp.bfloat16))
    return pl.pallas_call(
        functools.partial(attend_body, moment, has_next, len(earlier)),
        out_shape=tuple(shapes),
        in_specs=[vmem()] * len(operands),
        out_specs=(vmem(),) * len(shapes),
        compiler_params=pltpu.CompilerParams(vmem_limit_bytes=ATTEND_VMEM),
        cost_estimate=pl.CostEstimate(
            flops=4 * count * keys * channels,
            bytes_accessed=4 * keys * channels + 6 * count * channels,
            transcendentals=count * keys * channels // HD,
        ),
        name="attend",
    )(*operands)


def first_layer(raw, own, tiles, bias, hidden, gain):
    last = tiles - 1

    def move(tile, pairs):
        return lax.ppermute(tile, "tile", pairs)

    swap = [(i, i ^ 1) for i in range(tiles)]
    outward = [(0, 1), (last, last - 1)]
    outward += [(i, i + 2) for i in range(1, last, 2)] + [(i, i - 2) for i in range(2, tiles, 2)]
    relay = [(0, 0), (last, last)]
    relay += [(i, i + 1) for i in range(1, last, 2)] + [(i, i - 1) for i in range(2, tiles, 2)]
    first_raw = move(raw, outward)
    partner = move(own, swap)
    carry = partial_attend((0, 4), False, bias, hidden, gain, [own, partner])
    second = move(own, [(j, i) for i, j in outward])
    far_raw = move(first_raw, relay)
    first = split_keys_values(first_raw)
    partner_first = move(first, swap)
    partner_second = move(second, swap)
    tail = [first, second, partner_first, partner_second]
    carry = partial_attend((1, 2, 5, 6), False, bias, hidden, gain, tail, carry)
    far = split_keys_values(far_raw)
    pieces = partial_attend((3,), True, bias, hidden, gain, [far], carry)
    return [own, first, second, far, partner, partner_first, partner_second], pieces


def on_device(hidden, keys_values, q_gain, tile_mask):
    sections = lax.axis_size("section")
    rows = hidden.shape[0]
    raw = keys_values[0]
    own = split_keys_values(raw)
    bias = mask_bias(tile_mask, rows)
    window, pieces = first_layer(raw, own, lax.axis_size("tile"), bias, hidden, q_gain)
    kept, following = list(pieces[:PIECES]), list(pieces[PIECES:])
    for moment in range(1, sections):
        has_next = moment + 1 < sections
        others = [i for i in range(sections)[::-1] if i not in (moment - 1, moment)]
        cycle = [moment - 1, moment, *others]
        hop = list(zip(cycle, cycle[1:] + cycle[:1]))
        for p in range(PIECES):
            source = lax.ppermute(following[p], "section", hop)
            earlier = kept[:p] if not has_next and p + 1 == PIECES else ()
            results = attend(moment, has_next, bias, source, q_gain, window, kept[p], earlier)
            kept[p] = results[0]
            if has_next:
                following[p] = results[1]
    return kept[-1][None]


def solution(mesh):
    in_specs = (
        P("tile", None),
        P("section", "tile", None, None),
        P("section", None),
        P("tile", None),
    )
    out_specs = P("section", "tile", None)
    return jax.shard_map(
        on_device, mesh=mesh, in_specs=in_specs, out_specs=out_specs, check_vma=False
    )
```

time: 61.9 us -> 57.1 us (0.922)
  the two profiles are of different devices: /device:TPU:22 before, /device:TPU:20 now
where the time goes in v2:
time: 57.1 us; the launch traced here: 56.4 us
  waiting for transfers between devices  39.1 us (68%)
  starting transfers between devices  10.5 us (18%)
  Pallas kernels  5.4 us (9%)
  local copies, waits for them, and re-layouts  1.14 us (2%)
    ppermute x6, waiting for transfers between devices, move(): return lax.ppermute(tile, 'tile', pairs)  21.4 us
    ppermute x6, waiting for transfers between devices, on_device(): source = lax.ppermute(following[p], 'section', hop)  17.7 us
    ppermute x6, starting transfers between devices, on_device(): source = lax.ppermute(following[p], 'section', hop)  6.01 us
    ppermute x6, starting transfers between devices, move(): return lax.ppermute(tile, 'tile', pairs)  4.53 us
    pallas_call x6, Pallas kernels, attend(): pl.pallas_call(functools.partial(attend_body, moment, has_next, len(earli...  3.45 us
    pallas_call x3, Pallas kernels, split_keys_values(): pl.pallas_call(split_body, out_shape=jax.ShapeDtypeStruct((2, rows, chann...  1.32 us
  transfers between devices with their start and end apart: 12, of which 8 were waited for; matrix products, arithmetic and copies ran while one was open for 0% of the time, Pallas kernels for 8%

profile of v2, /device:TPU:20, one launch (start us, length us, event | category | flops | bytes accessed | tf_op | source)
XLA Modules:
  0.0 56.4 jit_solution(2365320892042525829)
XLA Ops:
  0.0 0.4 collective-permute-start
  0.5 0.0 copy-start.2
  0.5 1.1 %copy-done.2 = bf16[1,64,2,2560]{3,2,1,0:T(2,128)(2,1)S(1)} copy-done((bf16[1,64,2,2560]{3,2,1,0:T(2,128)(2,1)S(1)}, bf16[1,64,2,2560]{3,2,1,0:T(2,128)(2,1)}, u32[]{:S(2)}) %copy-start.2) | copy-done | bytes 655384
  1.6 0.4 split_kv.5.refs_0_
  2.0 0.0 copy-start.3
  2.0 1.6 %collective-permute-start.2 = (bf16[2,64,2560]{2,1,0:T(8,128)(2,1)S(1)}, bf16[2,64,2560]{2,1,0:T(8,128)(2,1)S(1)}, u32[]{:S(2)}, u32[]{:S(2)}) collective-permute-start(bf16[2,64,2560]{2,1,0:T(8,128)(2,1)S(1)} %split_kv.5.refs_0_), channel_id=1, source_target_pairs={{1,0},{6,7},{3,1},{5,3},{7,5},{0,2},{2,4},{4,6},{9,8},{14,15},{11,... | collective-permute-start | bytes 1966088 | tf_op jit(solution)/shard_map/ppermute | solution.py:274
  3.6 0.0 collective-permute-start.5
  3.6 12.6 %collective-permute-done.kv_ref = bf16[64,2,2560]{2,1,0:T(2,128)(2,1)S(1)} collective-permute-done((bf16[64,2,2560]{2,1,0:T(2,128)(2,1)}, bf16[64,2,2560]{2,1,0:T(2,128)(2,1)S(1)}, u32[]{:S(2)}, u32[]{:S(2)}) %collective-permute-start) | collective-permute-done | bytes 655392 | tf_op jit(solution)/shard_map/ppermute | solution.py:274
  16.3 0.0 copy-start
  16.3 0.4 split_kv.4.refs_0_.refs_1_
  16.7 0.0 copy-start.1
  16.7 1.9 %collective-permute-start.1 = (bf16[64,2,2560]{2,1,0:T(2,128)(2,1)S(1)}, bf16[64,2,2560]{2,1,0:T(2,128)(2,1)S(1)}, u32[]{:S(2)}, u32[]{:S(2)}) collective-permute-start(bf16[64,2,2560]{2,1,0:T(2,128)(2,1)S(1)} %collective-permute-done.kv_ref), channel_id=1, source_target_pairs={{0,0},{7,7},{1,2},{3,4},{5,6},{2,1},{4,3},{6,5},{8,8},{15,15},{9,1... | collective-permute-start | bytes 1966088 | tf_op jit(solution)/shard_map/ppermute | solution.py:274
  18.7 0.0 collective-permute-done.2.refs_1_.refs_2_
  18.7 0.1 collective-permute-start.4
  18.7 0.5 collective-permute-start.3
  19.2 0.0 copy-done.3
  19.2 0.6 %mask_bias.1.bias_ref = f32[448,128]{1,0:T(8,128)S(1)} custom-call(s32[1,7]{1,0:T(1,128)S(1)} %copy-done.3), custom_call_target="tpu_custom_call" | custom-call | tf_op jit(solution)/shard_map/mask_bias/pallas_call | solution.py:64
  19.8 0.0 collective-permute-done.5.refs_1_.refs_4_
  19.8 0.0 copy-done
  19.9 0.0 copy-done.1
  19.9 8.8 %collective-permute-done.1.kv_ref = bf16[64,2,2560]{2,1,0:T(2,128)(2,1)S(1)} collective-permute-done((bf16[64,2,2560]{2,1,0:T(2,128)(2,1)S(1)}, bf16[64,2,2560]{2,1,0:T(2,128)(2,1)S(1)}, u32[]{:S(2)}, u32[]{:S(2)}) %collective-permute-start.1) | collective-permute-done | bytes 655392 | tf_op jit(solution)/shard_map/ppermute | solution.py:274
  28.6 0.4 split_kv.3.refs_0_.refs_3_
  29.1 0.0 collective-permute-done.4.refs_3_.refs_6_
  29.1 0.0 collective-permute-done.3.refs_2_.refs_5_
  29.2 2.6 %collective-permute-start.9 = (bf16[32,2560]{1,0:T(8,128)(2,1)S(1)}, bf16[32,2560]{1,0:T(8,128)(2,1)S(1)}, u32[]{:S(2)}, u32[]{:S(2)}) collective-permute-start(bf16[32,2560]{1,0:T(8,128)(2,1)S(1)} %get-tuple-element.35), channel_id=1, source_target_pairs={{0,8},{8,24},{24,16},{16,0},{1,9},{9,25},{25,17},{17,1},{2,10},{10... | collective-permute-start | bytes 491528 | tf_op jit(solution)/shard_map/ppermute | solution.py:310
  31.8 0.1 collective-permute-start.6
  31.8 4.1 %collective-permute-done.9.src_ref = bf16[32,2560]{1,0:T(8,128)(2,1)S(1)} collective-permute-done((bf16[32,2560]{1,0:T(8,128)(2,1)S(1)}, bf16[32,2560]{1,0:T(8,128)(2,1)S(1)}, u32[]{:S(2)}, u32[]{:S(2)}) %collective-permute-start.9) | collective-permute-done | bytes 163872 | tf_op jit(solution)/shard_map/ppermute | solution.py:310
  35.9 1.0 %collective-permute-start.10 = (bf16[32,2560]{1,0:T(8,128)(2,1)S(1)}, bf16[32,2560]{1,0:T(8,128)(2,1)S(1)}, u32[]{:S(2)}, u32[]{:S(2)}) collective-permute-start(bf16[32,2560]{1,0:T(8,128)(2,1)S(1)} %get-tuple-element.37), channel_id=1, source_target_pairs={{8,16},{16,24},{24,0},{0,8},{9,17},{17,25},{25,1},{1,9},{10,18},{1... | collective-permute-start | bytes 491528 | tf_op jit(solution)/shard_map/ppermute | solution.py:310
  37.0 5.6 %collective-permute-done.6.src_ref = bf16[32,2560]{1,0:T(8,128)(2,1)S(1)} collective-permute-done((bf16[32,2560]{1,0:T(8,128)(2,1)S(1)}, bf16[32,2560]{1,0:T(8,128)(2,1)S(1)}, u32[]{:S(2)}, u32[]{:S(2)}) %collective-permute-start.6) | collective-permute-done | bytes 163872 | tf_op jit(solution)/shard_map/ppermute | solution.py:310
  42.6 0.1 collective-permute-start.7
  42.6 0.4 collective-permute-done.10.src_ref
  43.1 1.3 %attend.9 = (bf16[32,2560]{1,0:T(8,128)(2,1)S(1)}, bf16[32,2560]{1,0:T(8,128)(2,1)S(1)}) custom-call(f32[448,128]{1,0:T(8,128)S(1)} %mask_bias.1.bias_ref, bf16[32,2560]{1,0:T(8,128)(2,1)S(1)} %collective-permute-done.10.src_ref, f32[1,2560]{1,0:T(1,128)S(1)} %copy-done.1, bf16[2,64,2560]{2,1,0:T(8,128)(2,1)S(1)} %split_kv.5.refs_0_, ...), custom_call_target="tpu_custom_call" | custom-call | flops 146800640 | bytes 5079040 | tf_op jit(solution)/shard_map/attend/pallas_call | solution.py:255
  44.4 2.2 %collective-permute-start.11 = (bf16[32,2560]{1,0:T(8,128)(2,1)S(1)}, bf16[32,2560]{1,0:T(8,128)(2,1)S(1)}, u32[]{:S(2)}, u32[]{:S(2)}) collective-permute-start(bf16[32,2560]{1,0:T(8,128)(2,1)S(1)} %get-tuple-element.39), channel_id=1, source_target_pairs={{16,24},{24,8},{8,0},{0,16},{17,25},{25,9},{9,1},{1,17},{18,26},{2... | collective-permute-start | bytes 491528 | tf_op jit(solution)/shard_map/ppermute | solution.py:310
  46.6 2.3 %collective-permute-done.7.src_ref = bf16[32,2560]{1,0:T(8,128)(2,1)S(1)} collective-permute-done((bf16[32,2560]{1,0:T(8,128)(2,1)S(1)}, bf16[32,2560]{1,0:T(8,128)(2,1)S(1)}, u32[]{:S(2)}, u32[]{:S(2)}) %collective-permute-start.7) | collective-permute-done | bytes 163872 | tf_op jit(solution)/shard_map/ppermute | solution.py:310
  48.9 1.3 %attend.7 = (bf16[32,2560]{1,0:T(8,128)(2,1)S(1)}, bf16[32,2560]{1,0:T(8,128)(2,1)S(1)}) custom-call(f32[448,128]{1,0:T(8,128)S(1)} %mask_bias.1.bias_ref, bf16[32,2560]{1,0:T(8,128)(2,1)S(1)} %collective-permute-done.7.src_ref, f32[1,2560]{1,0:T(1,128)S(1)} %copy-done.1, bf16[2,64,2560]{2,1,0:T(8,128)(2,1)S(1)} %split_kv.5.refs_0_, ...), custom_call_target="tpu_custom_call" | custom-call | flops 146800640 | bytes 5079040 | tf_op jit(solution)/shard_map/attend/pallas_call | solution.py:255
  50.3 0.1 collective-permute-start.8
  50.3 0.8 %collective-permute-done.11.src_ref = bf16[32,2560]{1,0:T(8,128)(2,1)S(1)} collective-permute-done((bf16[32,2560]{1,0:T(8,128)(2,1)S(1)}, bf16[32,2560]{1,0:T(8,128)(2,1)S(1)}, u32[]{:S(2)}, u32[]{:S(2)}) %collective-permute-start.11) | collective-permute-done | bytes 163872 | tf_op jit(solution)/shard_map/ppermute | solution.py:310
  51.2 4.5 %collective-permute-done.8.src_ref = bf16[32,2560]{1,0:T(8,128)(2,1)S(1)} collective-permute-done((bf16[32,2560]{1,0:T(8,128)(2,1)S(1)}, bf16[32,2560]{1,0:T(8,128)(2,1)S(1)}, u32[]{:S(2)}, u32[]{:S(2)}) %collective-permute-start.8) | collective-permute-done | bytes 163872 | tf_op jit(solution)/shard_map/ppermute | solution.py:310
  55.6 0.7 %attend.11 = bf16[64,2560]{1,0:T(8,128)(2,1)} custom-call(f32[448,128]{1,0:T(8,128)S(1)} %mask_bias.1.bias_ref, bf16[32,2560]{1,0:T(8,128)(2,1)S(1)} %collective-permute-done.8.src_ref, f32[1,2560]{1,0:T(1,128)S(1)} %copy-done.1, bf16[2,64,2560]{2,1,0:T(8,128)(2,1)S(1)} %split_kv.5.refs_0_, bf16[2,64,2560]{2,1,0:T(8,128)(2,1)S(1)} %split_kv.4.refs_0_.refs_1_, ...), custom_call_target="tpu_custom_call" | custom-call | flops 146800640 | bytes 5079040 | tf_op jit(solution)/shard_map/attend/pallas_call | solution.py:255
  (6 shorter events, 0.1 us)
Async XLA Ops:
  0.0 16.3 %collective-permute-start = (bf16[64,2,2560]{2,1,0:T(2,128)(2,1)}, bf16[64,2,2560]{2,1,0:T(2,128)(2,1)S(1)}, u32[]{:S(2)}, u32[]{:S(2)}) collective-permute-start(bf16[64,2,2560]{2,1,0:T(2,128)(2,1)} %bitcast.2), channel_id=1, source_target_pairs={{0,1},{7,6},{1,3},{3,5},{5,7},{2,0},{4,2},{6,4},{8,9},{15,14},{9,1... | collective-permute-start | bytes 1966088 | tf_op jit(solution)/shard_map/ppermute | solution.py:274
  0.5 1.1 %copy-start.2 = (bf16[1,64,2,2560]{3,2,1,0:T(2,128)(2,1)S(1)}, bf16[1,64,2,2560]{3,2,1,0:T(2,128)(2,1)}, u32[]{:S(2)}) copy-start(bf16[1,64,2,2560]{3,2,1,0:T(2,128)(2,1)} %param.5) | copy-start | bytes 1966084
  2.0 17.2 %copy-start.3 = (s32[1,7]{1,0:T(1,128)S(1)}, s32[1,7]{1,0:T(1,128)}, u32[]{:S(2)}) copy-start(s32[1,7]{1,0:T(1,128)} %mask_ref.1) | copy-start | bytes 88
  2.0 16.6 %collective-permute-start.2 = (bf16[2,64,2560]{2,1,0:T(8,128)(2,1)S(1)}, bf16[2,64,2560]{2,1,0:T(8,128)(2,1)S(1)}, u32[]{:S(2)}, u32[]{:S(2)}) collective-permute-start(bf16[2,64,2560]{2,1,0:T(8,128)(2,1)S(1)} %split_kv.5.refs_0_), channel_id=1, source_target_pairs={{1,0},{6,7},{3,1},{5,3},{7,5},{0,2},{2,4},{4,6},{9,8},{14,15},{11,... | collective-permute-start | bytes 1966088 | tf_op jit(solution)/shard_map/ppermute | solution.py:274
  3.6 16.2 %collective-permute-start.5 = (bf16[2,64,2560]{2,1,0:T(8,128)(2,1)S(1)}, bf16[2,64,2560]{2,1,0:T(8,128)(2,1)S(1)}, u32[]{:S(2)}, u32[]{:S(2)}) collective-permute-start(bf16[2,64,2560]{2,1,0:T(8,128)(2,1)S(1)} %split_kv.5.refs_0_), channel_id=1, source_target_pairs={{0,1},{1,0},{2,3},{3,2},{4,5},{5,4},{6,7},{7,6},{8,9},{9,8},{10,11... | collective-permute-start | bytes 1966088 | tf_op jit(solution)/shard_map/ppermute | solution.py:274
  16.3 3.6 %copy-start = (bf16[64,2560]{1,0:T(8,128)(2,1)S(1)}, bf16[64,2560]{1,0:T(8,128)(2,1)}, u32[]{:S(2)}) copy-start(bf16[64,2560]{1,0:T(8,128)(2,1)} %src_ref.5) | copy-start | bytes 983044
  16.7 3.1 %copy-start.1 = (f32[1,2560]{1,0:T(1,128)S(1)}, f32[1,2560]{1,0:T(1,128)}, u32[]{:S(2)}) copy-start(f32[1,2560]{1,0:T(1,128)} %gain_ref.17) | copy-start | bytes 30724
  16.7 11.9 %collective-permute-start.1 = (bf16[64,2,2560]{2,1,0:T(2,128)(2,1)S(1)}, bf16[64,2,2560]{2,1,0:T(2,128)(2,1)S(1)}, u32[]{:S(2)}, u32[]{:S(2)}) collective-permute-start(bf16[64,2,2560]{2,1,0:T(2,128)(2,1)S(1)} %collective-permute-done.kv_ref), channel_id=1, source_target_pairs={{0,0},{7,7},{1,2},{3,4},{5,6},{2,1},{4,3},{6,5},{8,8},{15,15},{9,1... | collective-permute-start | bytes 1966088 | tf_op jit(solution)/shard_map/ppermute | solution.py:274
  18.7 10.4 %collective-permute-start.4 = (bf16[2,64,2560]{2,1,0:T(8,128)(2,1)S(1)}, bf16[2,64,2560]{2,1,0:T(8,128)(2,1)S(1)}, u32[]{:S(2)}, u32[]{:S(2)}) collective-permute-start(bf16[2,64,2560]{2,1,0:T(8,128)(2,1)S(1)} %collective-permute-done.2.refs_1_.refs_2_), channel_id=1, source_target_pairs={{0,1},{1,0},{2,3},{3,2},{4,5},{5,4},{6,7},{7,6},{8,9},{9,8},{10,11... | collective-permute-start | bytes 1966088 | tf_op jit(solution)/shard_map/ppermute | solution.py:274
  18.7 10.3 %collective-permute-start.3 = (bf16[2,64,2560]{2,1,0:T(8,128)(2,1)S(1)}, bf16[2,64,2560]{2,1,0:T(8,128)(2,1)S(1)}, u32[]{:S(2)}, u32[]{:S(2)}) collective-permute-start(bf16[2,64,2560]{2,1,0:T(8,128)(2,1)S(1)} %split_kv.4.refs_0_.refs_1_), channel_id=1, source_target_pairs={{0,1},{1,0},{2,3},{3,2},{4,5},{5,4},{6,7},{7,6},{8,9},{9,8},{10,11... | collective-permute-start | bytes 1966088 | tf_op jit(solution)/shard_map/ppermute | solution.py:274
  29.2 6.8 %collective-permute-start.9 = (bf16[32,2560]{1,0:T(8,128)(2,1)S(1)}, bf16[32,2560]{1,0:T(8,128)(2,1)S(1)}, u32[]{:S(2)}, u32[]{:S(2)}) collective-permute-start(bf16[32,2560]{1,0:T(8,128)(2,1)S(1)} %get-tuple-element.35), channel_id=1, source_target_pairs={{0,8},{8,24},{24,16},{16,0},{1,9},{9,25},{25,17},{17,1},{2,10},{10... | collective-permute-start | bytes 491528 | tf_op jit(solution)/shard_map/ppermute | solution.py:310
  31.8 10.8 %collective-permute-start.6 = (bf16[32,2560]{1,0:T(8,128)(2,1)S(1)}, bf16[32,2560]{1,0:T(8,128)(2,1)S(1)}, u32[]{:S(2)}, u32[]{:S(2)}) collective-permute-start(bf16[32,2560]{1,0:T(8,128)(2,1)S(1)} %get-tuple-element.29), channel_id=1, source_target_pairs={{0,8},{8,24},{24,16},{16,0},{1,9},{9,25},{25,17},{17,1},{2,10},{10... | collective-permute-start | bytes 491528 | tf_op jit(solution)/shard_map/ppermute | solution.py:310
  35.9 7.1 %collective-permute-start.10 = (bf16[32,2560]{1,0:T(8,128)(2,1)S(1)}, bf16[32,2560]{1,0:T(8,128)(2,1)S(1)}, u32[]{:S(2)}, u32[]{:S(2)}) collective-permute-start(bf16[32,2560]{1,0:T(8,128)(2,1)S(1)} %get-tuple-element.37), channel_id=1, source_target_pairs={{8,16},{16,24},{24,0},{0,8},{9,17},{17,25},{25,1},{1,9},{10,18},{1... | collective-permute-start | bytes 491528 | tf_op jit(solution)/shard_map/ppermute | solution.py:310
  42.6 6.4 %collective-permute-start.7 = (bf16[32,2560]{1,0:T(8,128)(2,1)S(1)}, bf16[32,2560]{1,0:T(8,128)(2,1)S(1)}, u32[]{:S(2)}, u32[]{:S(2)}) collective-permute-start(bf16[32,2560]{1,0:T(8,128)(2,1)S(1)} %get-tuple-element.31), channel_id=1, source_target_pairs={{8,16},{16,24},{24,0},{0,8},{9,17},{17,25},{25,1},{1,9},{10,18},{1... | collective-permute-start | bytes 491528 | tf_op jit(solution)/shard_map/ppermute | solution.py:310
  44.4 6.7 %collective-permute-start.11 = (bf16[32,2560]{1,0:T(8,128)(2,1)S(1)}, bf16[32,2560]{1,0:T(8,128)(2,1)S(1)}, u32[]{:S(2)}, u32[]{:S(2)}) collective-permute-start(bf16[32,2560]{1,0:T(8,128)(2,1)S(1)} %get-tuple-element.39), channel_id=1, source_target_pairs={{16,24},{24,8},{8,0},{0,16},{17,25},{25,9},{9,1},{1,17},{18,26},{2... | collective-permute-start | bytes 491528 | tf_op jit(solution)/shard_map/ppermute | solution.py:310
  50.3 5.4 %collective-permute-start.8 = (bf16[32,2560]{1,0:T(8,128)(2,1)S(1)}, bf16[32,2560]{1,0:T(8,128)(2,1)S(1)}, u32[]{:S(2)}, u32[]{:S(2)}) collective-permute-start(bf16[32,2560]{1,0:T(8,128)(2,1)S(1)} %get-tuple-element.33), channel_id=1, source_target_pairs={{16,24},{24,8},{8,0},{0,16},{17,25},{25,9},{9,1},{1,17},{18,26},{2... | collective-permute-start | bytes 491528 | tf_op jit(solution)/shard_map/ppermute | solution.py:310

commit v3 on v2

--- a/solution.py
+++ b/solution.py
@@ -13,7 +13,7 @@
 LANES = 128
 NEG = -1e30
 SCALE = HD**-0.5 * 1.4426950408889634
-PIECES = 2
+PIECES = 4
 SLOTS = (0, 2, -2, -3, 1, -1, 3)
 ATTEND_VMEM = 24 << 20
 SPLIT_VMEM = 8 << 20
@@ -269,9 +269,17 @@
 
 def first_layer(raw, own, tiles, bias, hidden, gain):
     last = tiles - 1
+    sections = lax.axis_size("section")
 
     def move(tile, pairs):
-        return lax.ppermute(tile, "tile", pairs)
+        return lax.ppermute(tile, ("section", "tile"), on_all(pairs))
+
+    def on_all(pairs):
+        return [
+            (s * tiles + i, (s if i != j else (s ^ 1) % sections) * tiles + j)
+            for s in range(sections)
+            for i, j in pairs
+        ]
 
     swap = [(i, i ^ 1) for i in range(tiles)]
     outward = [(0, 1), (last, last - 1)]

time: 57.1 us -> 59.1 us (1.035)
  the two profiles are of different devices: /device:TPU:20 before, /device:TPU:0 now
where the time goes in v3:
time: 59.1 us; the launch traced here: 58.9 us
  waiting for transfers between devices  29.9 us (51%)
  starting transfers between devices  22.1 us (37%)
  Pallas kernels  5.62 us (10%)
  local copies, waits for them, and re-layouts  1.1 us (2%)
    ppermute x6, waiting for transfers between devices, move(): return lax.ppermute(tile, ('section', 'tile'), on_all(pairs))  18.9 us
    ppermute x12, starting transfers between devices, on_device(): source = lax.ppermute(following[p], 'section', hop)  16.1 us
    ppermute x12, waiting for transfers between devices, on_device(): source = lax.ppermute(following[p], 'section', hop)  11 us
    ppermute x6, starting transfers between devices, move(): return lax.ppermute(tile, ('section', 'tile'), on_all(pairs))  6.07 us
    pallas_call x3, Pallas kernels, partial_attend(): pl.pallas_call(functools.partial(partial_body, slots, bool(carry), last),...  2.87 us
    pallas_call x3, Pallas kernels, split_keys_values(): pl.pallas_call(split_body, out_shape=jax.ShapeDtypeStruct((2, rows, chann...  1.33 us
  transfers between devices with their start and end apart: 18, of which 8 were waited for; matrix products, arithmetic and copies ran while one was open for 0% of the time, Pallas kernels for 5%

profile of v3, /device:TPU:0, one launch (start us, length us, event | category | flops | bytes accessed | tf_op | source)
XLA Modules:
  0.0 58.9 jit_solution(2135135541572808712)
XLA Ops:
  0.0 0.5 collective-permute-start
  0.5 1.1 %copy-done.2 = bf16[1,64,2,2560]{3,2,1,0:T(2,128)(2,1)S(1)} copy-done((bf16[1,64,2,2560]{3,2,1,0:T(2,128)(2,1)S(1)}, bf16[1,64,2,2560]{3,2,1,0:T(2,128)(2,1)}, u32[]{:S(2)}) %copy-start.2) | copy-done | bytes 655384
  1.6 0.4 split_kv.5.refs_0_
  2.0 0.0 copy-start.3
  2.0 2.6 %collective-permute-start.2 = (bf16[2,64,2560]{2,1,0:T(8,128)(2,1)S(1)}, bf16[2,64,2560]{2,1,0:T(8,128)(2,1)S(1)}, u32[]{:S(2)}, u32[]{:S(2)}) collective-permute-start(bf16[2,64,2560]{2,1,0:T(8,128)(2,1)S(1)} %split_kv.5.refs_0_), channel_id=1, source_target_pairs={{1,0},{6,7},{3,1},{5,3},{7,5},{0,2},{2,4},{4,6},{9,8},{14,15},{11,... | collective-permute-start | bytes 1966088 | tf_op jit(solution)/shard_map/ppermute | solution.py:275
  4.7 0.0 collective-permute-start.5
  4.7 12.2 %collective-permute-done.kv_ref = bf16[64,2,2560]{2,1,0:T(2,128)(2,1)S(1)} collective-permute-done((bf16[64,2,2560]{2,1,0:T(2,128)(2,1)}, bf16[64,2,2560]{2,1,0:T(2,128)(2,1)S(1)}, u32[]{:S(2)}, u32[]{:S(2)}) %collective-permute-start) | collective-permute-done | bytes 655392 | tf_op jit(solution)/shard_map/ppermute | solution.py:275
  16.9 0.4 split_kv.4.refs_0_.refs_1_
  17.3 0.0 copy-start.1
  17.3 2.5 %collective-permute-start.1 = (bf16[64,2,2560]{2,1,0:T(2,128)(2,1)S(1)}, bf16[64,2,2560]{2,1,0:T(2,128)(2,1)S(1)}, u32[]{:S(2)}, u32[]{:S(2)}) collective-permute-start(bf16[64,2,2560]{2,1,0:T(2,128)(2,1)S(1)} %collective-permute-done.kv_ref), channel_id=1, source_target_pairs={{0,8},{7,15},{1,2},{3,4},{5,6},{2,1},{4,3},{6,5},{8,0},{15,7},{9,1... | collective-permute-start | bytes 1966088 | tf_op jit(solution)/shard_map/ppermute | solution.py:275
  19.8 0.0 collective-permute-done.2.refs_1_.refs_2_
  19.8 0.2 collective-permute-start.4
  20.0 0.3 collective-permute-start.3
  20.3 0.6 mask_bias.1.bias_ref
  20.9 0.0 collective-permute-done.5.refs_1_.refs_4_
  20.9 0.0 copy-done
  20.9 0.8 %partial_attend.3 = (f32[10,128]{1,0:T(8,128)S(1)}, f32[10,128]{1,0:T(8,128)S(1)}, f32[64,2560]{1,0:T(8,128)S(1)}) custom-call(f32[448,128]{1,0:T(8,128)S(1)} %mask_bias.1.bias_ref, bf16[64,2560]{1,0:T(8,128)(2,1)S(1)} %copy-done, f32[1,2560]{1,0:T(1,128)S(1)} %copy-done.1, bf16[2,64,2560]{2,1,0:T(8,128)(2,1)S(1)} %split_kv.5.refs_0_, ...), custom_call_target="tpu_custom_call" | custom-call | flops 83886080 | bytes 2293760 | tf_op jit(solution)/shard_map/partial_attend/pallas_call | solution.py:205
  21.7 6.7 %collective-permute-done.1.kv_ref = bf16[64,2,2560]{2,1,0:T(2,128)(2,1)S(1)} collective-permute-done((bf16[64,2,2560]{2,1,0:T(2,128)(2,1)S(1)}, bf16[64,2,2560]{2,1,0:T(2,128)(2,1)S(1)}, u32[]{:S(2)}, u32[]{:S(2)}) %collective-permute-start.1) | collective-permute-done | bytes 655392 | tf_op jit(solution)/shard_map/ppermute | solution.py:275
  28.3 0.4 split_kv.3.refs_0_.refs_3_
  28.8 0.0 collective-permute-done.4.refs_3_.refs_6_
  28.8 0.0 collective-permute-done.3.refs_2_.refs_5_
  28.8 1.1 %partial_attend.4 = (f32[10,128]{1,0:T(8,128)S(1)}, f32[10,128]{1,0:T(8,128)S(1)}, f32[64,2560]{1,0:T(8,128)S(1)}) custom-call(f32[448,128]{1,0:T(8,128)S(1)} %mask_bias.1.bias_ref, bf16[64,2560]{1,0:T(8,128)(2,1)S(1)} %copy-done, f32[1,2560]{1,0:T(1,128)S(1)} %copy-done.1, bf16[2,64,2560]{2,1,0:T(8,128)(2,1)S(1)} %split_kv.4.refs_0_.refs_1_, ...), custom_call_target="tpu_custom_call" | custom-call | flops 167772160 | bytes 3604480 | tf_op jit(solution)/shard_map/partial_attend/pallas_call | solution.py:205
  29.9 1.0 %partial_attend.5 = (bf16[16,2560]{1,0:T(8,128)(2,1)S(1)}, bf16[16,2560]{1,0:T(8,128)(2,1)S(1)}, bf16[16,2560]{1,0:T(8,128)(2,1)S(1)}, bf16[16,2560]{1,0:T(8,128...) custom-call(f32[448,128]{1,0:T(8,128)S(1)} %mask_bias.1.bias_ref, ...), custom_call_target="tpu_custom_call" | custom-call | flops 41943040 | bytes 1638400 | tf_op jit(solution)/shard_map/partial_attend/pallas_call | solution.py:205
  30.9 0.1 collective-permute-start.9
  31.0 1.5 %collective-permute-start.12 = (bf16[16,2560]{1,0:T(8,128)(2,1)S(1)}, bf16[16,2560]{1,0:T(8,128)(2,1)S(1)}, u32[]{:S(2)}, u32[]{:S(2)}) collective-permute-start(bf16[16,2560]{1,0:T(8,128)(2,1)S(1)} %get-tuple-element.53), channel_id=1, source_target_pairs={{0,8},{8,24},{24,16},{16,0},{1,9},{9,25},{25,17},{17,1},{2,10},{10... | collective-permute-start | bytes 245768 | tf_op jit(solution)/shard_map/ppermute | solution.py:318
  32.4 0.5 collective-permute-start.15
  33.0 2.0 %collective-permute-start.6 = (bf16[16,2560]{1,0:T(8,128)(2,1)S(1)}, bf16[16,2560]{1,0:T(8,128)(2,1)S(1)}, u32[]{:S(2)}, u32[]{:S(2)}) collective-permute-start(bf16[16,2560]{1,0:T(8,128)(2,1)S(1)} %get-tuple-element.41), channel_id=1, source_target_pairs={{0,8},{8,24},{24,16},{16,0},{1,9},{9,25},{25,17},{17,1},{2,10},{10... | collective-permute-start | bytes 245768 | tf_op jit(solution)/shard_map/ppermute | solution.py:318
  35.0 1.3 %collective-permute-done.9.src_ref = bf16[16,2560]{1,0:T(8,128)(2,1)S(1)} collective-permute-done((bf16[16,2560]{1,0:T(8,128)(2,1)S(1)}, bf16[16,2560]{1,0:T(8,128)(2,1)S(1)}, u32[]{:S(2)}, u32[]{:S(2)}) %collective-permute-start.9) | collective-permute-done | bytes 81952 | tf_op jit(solution)/shard_map/ppermute | solution.py:318
  36.3 1.5 %collective-permute-start.10 = (bf16[16,2560]{1,0:T(8,128)(2,1)S(1)}, bf16[16,2560]{1,0:T(8,128)(2,1)S(1)}, u32[]{:S(2)}, u32[]{:S(2)}) collective-permute-start(bf16[16,2560]{1,0:T(8,128)(2,1)S(1)} %get-tuple-element.49), channel_id=1, source_target_pairs={{8,16},{16,24},{24,0},{0,8},{9,17},{17,25},{25,1},{1,9},{10,18},{1... | collective-permute-start | bytes 245768 | tf_op jit(solution)/shard_map/ppermute | solution.py:318
  37.8 0.2 collective-permute-done.12.src_ref
  38.0 1.5 %collective-permute-start.13 = (bf16[16,2560]{1,0:T(8,128)(2,1)S(1)}, bf16[16,2560]{1,0:T(8,128)(2,1)S(1)}, u32[]{:S(2)}, u32[]{:S(2)}) collective-permute-start(bf16[16,2560]{1,0:T(8,128)(2,1)S(1)} %get-tuple-element.55), channel_id=1, source_target_pairs={{8,16},{16,24},{24,0},{0,8},{9,17},{17,25},{25,1},{1,9},{10,18},{1... | collective-permute-start | bytes 245768 | tf_op jit(solution)/shard_map/ppermute | solution.py:318
  39.6 1.0 %collective-permute-done.15.src_ref = bf16[16,2560]{1,0:T(8,128)(2,1)S(1)} collective-permute-done((bf16[16,2560]{1,0:T(8,128)(2,1)S(1)}, bf16[16,2560]{1,0:T(8,128)(2,1)S(1)}, u32[]{:S(2)}, u32[]{:S(2)}) %collective-permute-start.15) | collective-permute-done | bytes 81952 | tf_op jit(solution)/shard_map/ppermute | solution.py:318
  40.6 0.7 %collective-permute-start.16 = (bf16[16,2560]{1,0:T(8,128)(2,1)S(1)}, bf16[16,2560]{1,0:T(8,128)(2,1)S(1)}, u32[]{:S(2)}, u32[]{:S(2)}) collective-permute-start(bf16[16,2560]{1,0:T(8,128)(2,1)S(1)} %get-tuple-element.61), channel_id=1, source_target_pairs={{8,16},{16,24},{24,0},{0,8},{9,17},{17,25},{25,1},{1,9},{10,18},{1... | collective-permute-start | bytes 245768 | tf_op jit(solution)/shard_map/ppermute | solution.py:318
  41.3 5.5 %collective-permute-done.6.src_ref = bf16[16,2560]{1,0:T(8,128)(2,1)S(1)} collective-permute-done((bf16[16,2560]{1,0:T(8,128)(2,1)S(1)}, bf16[16,2560]{1,0:T(8,128)(2,1)S(1)}, u32[]{:S(2)}, u32[]{:S(2)}) %collective-permute-start.6) | collective-permute-done | bytes 81952 | tf_op jit(solution)/shard_map/ppermute | solution.py:318
  46.8 0.0 collective-permute-start.7
  46.9 0.0 collective-permute-done.10.src_ref
  46.9 1.1 %collective-permute-start.11 = (bf16[16,2560]{1,0:T(8,128)(2,1)S(1)}, bf16[16,2560]{1,0:T(8,128)(2,1)S(1)}, u32[]{:S(2)}, u32[]{:S(2)}) collective-permute-start(bf16[16,2560]{1,0:T(8,128)(2,1)S(1)} %get-tuple-element.51), channel_id=1, source_target_pairs={{16,24},{24,8},{8,0},{0,16},{17,25},{25,9},{9,1},{1,17},{18,26},{2... | collective-permute-start | bytes 245768 | tf_op jit(solution)/shard_map/ppermute | solution.py:318
  48.0 0.0 collective-permute-done.13.src_ref
  48.0 3.9 %collective-permute-start.14 = (bf16[16,2560]{1,0:T(8,128)(2,1)S(1)}, bf16[16,2560]{1,0:T(8,128)(2,1)S(1)}, u32[]{:S(2)}, u32[]{:S(2)}) collective-permute-start(bf16[16,2560]{1,0:T(8,128)(2,1)S(1)} %get-tuple-element.57), channel_id=1, source_target_pairs={{16,24},{24,8},{8,0},{0,16},{17,25},{25,9},{9,1},{1,17},{18,26},{2... | collective-permute-start | bytes 245768 | tf_op jit(solution)/shard_map/ppermute | solution.py:318
  51.9 0.0 collective-permute-done.16.src_ref
  51.9 1.7 %collective-permute-start.17 = (bf16[16,2560]{1,0:T(8,128)(2,1)S(1)}, bf16[16,2560]{1,0:T(8,128)(2,1)S(1)}, u32[]{:S(2)}, u32[]{:S(2)}) collective-permute-start(bf16[16,2560]{1,0:T(8,128)(2,1)S(1)} %get-tuple-element.63), channel_id=1, source_target_pairs={{16,24},{24,8},{8,0},{0,16},{17,25},{25,9},{9,1},{1,17},{18,26},{2... | collective-permute-start | bytes 245768 | tf_op jit(solution)/shard_map/ppermute | solution.py:318
  53.6 0.0 collective-permute-done.7.src_ref
  53.7 1.5 %collective-permute-start.8 = (bf16[16,2560]{1,0:T(8,128)(2,1)S(1)}, bf16[16,2560]{1,0:T(8,128)(2,1)S(1)}, u32[]{:S(2)}, u32[]{:S(2)}) collective-permute-start(bf16[16,2560]{1,0:T(8,128)(2,1)S(1)} %get-tuple-element.45), channel_id=1, source_target_pairs={{16,24},{24,8},{8,0},{0,16},{17,25},{25,9},{9,1},{1,17},{18,26},{2... | collective-permute-start | bytes 245768 | tf_op jit(solution)/shard_map/ppermute | solution.py:318
  55.2 0.0 collective-permute-done.11.src_ref
  55.2 0.0 collective-permute-done.14.src_ref
  55.2 1.4 %collective-permute-done.17.src_ref = bf16[16,2560]{1,0:T(8,128)(2,1)S(1)} collective-permute-done((bf16[16,2560]{1,0:T(8,128)(2,1)S(1)}, bf16[16,2560]{1,0:T(8,128)(2,1)S(1)}, u32[]{:S(2)}, u32[]{:S(2)}) %collective-permute-start.17) | collective-permute-done | bytes 81952 | tf_op jit(solution)/shard_map/ppermute | solution.py:318
  56.6 1.5 %collective-permute-done.8.src_ref = bf16[16,2560]{1,0:T(8,128)(2,1)S(1)} collective-permute-done((bf16[16,2560]{1,0:T(8,128)(2,1)S(1)}, bf16[16,2560]{1,0:T(8,128)(2,1)S(1)}, u32[]{:S(2)}, u32[]{:S(2)}) %collective-permute-start.8) | collective-permute-done | bytes 81952 | tf_op jit(solution)/shard_map/ppermute | solution.py:318
  58.2 0.7 %attend.23 = bf16[64,2560]{1,0:T(8,128)(2,1)} custom-call(f32[448,128]{1,0:T(8,128)S(1)} %mask_bias.1.bias_ref, bf16[16,2560]{1,0:T(8,128)(2,1)S(1)} %collective-permute-done.8.src_ref, f32[1,2560]{1,0:T(1,128)S(1)} %copy-done.1, bf16[2,64,2560]{2,1,0:T(8,128)(2,1)S(1)} %split_kv.5.refs_0_, bf16[2,64,2560]{2,1,0:T(8,128)(2,1)S(1)} %split_kv.4.refs_0_.refs_1_, ...), custom_call_target="tpu_custom_call" | custom-call | flops 73400320 | bytes 4833280 | tf_op jit(solution)/shard_map/attend/pallas_call | solution.py:255
  (15 shorter events, 0.1 us)
Async XLA Ops:
  0.0 16.9 %collective-permute-start = (bf16[64,2,2560]{2,1,0:T(2,128)(2,1)}, bf16[64,2,2560]{2,1,0:T(2,128)(2,1)S(1)}, u32[]{:S(2)}, u32[]{:S(2)}) collective-permute-start(bf16[64,2,2560]{2,1,0:T(2,128)(2,1)} %bitcast.2), channel_id=1, source_target_pairs={{0,1},{7,6},{1,3},{3,5},{5,7},{2,0},{4,2},{6,4},{8,9},{15,14},{9,1... | collective-permute-start | bytes 1966088 | tf_op jit(solution)/shard_map/ppermute | solution.py:275
  0.5 1.1 %copy-start.2 = (bf16[1,64,2,2560]{3,2,1,0:T(2,128)(2,1)S(1)}, bf16[1,64,2,2560]{3,2,1,0:T(2,128)(2,1)}, u32[]{:S(2)}) copy-start(bf16[1,64,2,2560]{3,2,1,0:T(2,128)(2,1)} %param.5) | copy-start | bytes 1966084
  2.0 18.3 %copy-start.3 = (s32[1,7]{1,0:T(1,128)S(1)}, s32[1,7]{1,0:T(1,128)}, u32[]{:S(2)}) copy-start(s32[1,7]{1,0:T(1,128)} %mask_ref.1) | copy-start | bytes 88
  2.0 17.7 %collective-permute-start.2 = (bf16[2,64,2560]{2,1,0:T(8,128)(2,1)S(1)}, bf16[2,64,2560]{2,1,0:T(8,128)(2,1)S(1)}, u32[]{:S(2)}, u32[]{:S(2)}) collective-permute-start(bf16[2,64,2560]{2,1,0:T(8,128)(2,1)S(1)} %split_kv.5.refs_0_), channel_id=1, source_target_pairs={{1,0},{6,7},{3,1},{5,3},{7,5},{0,2},{2,4},{4,6},{9,8},{14,15},{11,... | collective-permute-start | bytes 1966088 | tf_op jit(solution)/shard_map/ppermute | solution.py:275
  4.7 16.2 %collective-permute-start.5 = (bf16[2,64,2560]{2,1,0:T(8,128)(2,1)S(1)}, bf16[2,64,2560]{2,1,0:T(8,128)(2,1)S(1)}, u32[]{:S(2)}, u32[]{:S(2)}) collective-permute-start(bf16[2,64,2560]{2,1,0:T(8,128)(2,1)S(1)} %split_kv.5.refs_0_), channel_id=1, source_target_pairs={{0,1},{1,0},{2,3},{3,2},{4,5},{5,4},{6,7},{7,6},{8,9},{9,8},{10,11... | collective-permute-start | bytes 1966088 | tf_op jit(solution)/shard_map/ppermute | solution.py:275
  16.9 4.0 %copy-start = (bf16[64,2560]{1,0:T(8,128)(2,1)S(1)}, bf16[64,2560]{1,0:T(8,128)(2,1)}, u32[]{:S(2)}) copy-start(bf16[64,2560]{1,0:T(8,128)(2,1)} %src_ref.5) | copy-start | bytes 983044
  17.3 3.6 %copy-start.1 = (f32[1,2560]{1,0:T(1,128)S(1)}, f32[1,2560]{1,0:T(1,128)}, u32[]{:S(2)}) copy-start(f32[1,2560]{1,0:T(1,128)} %gain_ref.29) | copy-start | bytes 30724
  17.3 11.0 %collective-permute-start.1 = (bf16[64,2,2560]{2,1,0:T(2,128)(2,1)S(1)}, bf16[64,2,2560]{2,1,0:T(2,128)(2,1)S(1)}, u32[]{:S(2)}, u32[]{:S(2)}) collective-permute-start(bf16[64,2,2560]{2,1,0:T(2,128)(2,1)S(1)} %collective-permute-done.kv_ref), channel_id=1, source_target_pairs={{0,8},{7,15},{1,2},{3,4},{5,6},{2,1},{4,3},{6,5},{8,0},{15,7},{9,1... | collective-permute-start | bytes 1966088 | tf_op jit(solution)/shard_map/ppermute | solution.py:275
  19.8 9.0 %collective-permute-start.4 = (bf16[2,64,2560]{2,1,0:T(8,128)(2,1)S(1)}, bf16[2,64,2560]{2,1,0:T(8,128)(2,1)S(1)}, u32[]{:S(2)}, u32[]{:S(2)}) collective-permute-start(bf16[2,64,2560]{2,1,0:T(8,128)(2,1)S(1)} %collective-permute-done.2.refs_1_.refs_2_), channel_id=1, source_target_pairs={{0,1},{1,0},{2,3},{3,2},{4,5},{5,4},{6,7},{7,6},{8,9},{9,8},{10,11... | collective-permute-start | bytes 1966088 | tf_op jit(solution)/shard_map/ppermute | solution.py:275
  20.0 8.8 %collective-permute-start.3 = (bf16[2,64,2560]{2,1,0:T(8,128)(2,1)S(1)}, bf16[2,64,2560]{2,1,0:T(8,128)(2,1)S(1)}, u32[]{:S(2)}, u32[]{:S(2)}) collective-permute-start(bf16[2,64,2560]{2,1,0:T(8,128)(2,1)S(1)} %split_kv.4.refs_0_.refs_1_), channel_id=1, source_target_pairs={{0,1},{1,0},{2,3},{3,2},{4,5},{5,4},{6,7},{7,6},{8,9},{9,8},{10,11... | collective-permute-start | bytes 1966088 | tf_op jit(solution)/shard_map/ppermute | solution.py:275
  30.9 5.4 %collective-permute-start.9 = (bf16[16,2560]{1,0:T(8,128)(2,1)S(1)}, bf16[16,2560]{1,0:T(8,128)(2,1)S(1)}, u32[]{:S(2)}, u32[]{:S(2)}) collective-permute-start(bf16[16,2560]{1,0:T(8,128)(2,1)S(1)} %get-tuple-element.47), channel_id=1, source_target_pairs={{0,8},{8,24},{24,16},{16,0},{1,9},{9,25},{25,17},{17,1},{2,10},{10... | collective-permute-start | bytes 245768 | tf_op jit(solution)/shard_map/ppermute | solution.py:318
  31.0 7.1 %collective-permute-start.12 = (bf16[16,2560]{1,0:T(8,128)(2,1)S(1)}, bf16[16,2560]{1,0:T(8,128)(2,1)S(1)}, u32[]{:S(2)}, u32[]{:S(2)}) collective-permute-start(bf16[16,2560]{1,0:T(8,128)(2,1)S(1)} %get-tuple-element.53), channel_id=1, source_target_pairs={{0,8},{8,24},{24,16},{16,0},{1,9},{9,25},{25,17},{17,1},{2,10},{10... | collective-permute-start | bytes 245768 | tf_op jit(solution)/shard_map/ppermute | solution.py:318
  32.4 8.2 %collective-permute-start.15 = (bf16[16,2560]{1,0:T(8,128)(2,1)S(1)}, bf16[16,2560]{1,0:T(8,128)(2,1)S(1)}, u32[]{:S(2)}, u32[]{:S(2)}) collective-permute-start(bf16[16,2560]{1,0:T(8,128)(2,1)S(1)} %get-tuple-element.59), channel_id=1, source_target_pairs={{0,8},{8,24},{24,16},{16,0},{1,9},{9,25},{25,17},{17,1},{2,10},{10... | collective-permute-start | bytes 245768 | tf_op jit(solution)/shard_map/ppermute | solution.py:318
  33.0 13.9 %collective-permute-start.6 = (bf16[16,2560]{1,0:T(8,128)(2,1)S(1)}, bf16[16,2560]{1,0:T(8,128)(2,1)S(1)}, u32[]{:S(2)}, u32[]{:S(2)}) collective-permute-start(bf16[16,2560]{1,0:T(8,128)(2,1)S(1)} %get-tuple-element.41), channel_id=1, source_target_pairs={{0,8},{8,24},{24,16},{16,0},{1,9},{9,25},{25,17},{17,1},{2,10},{10... | collective-permute-start | bytes 245768 | tf_op jit(solution)/shard_map/ppermute | solution.py:318
  36.3 10.6 %collective-permute-start.10 = (bf16[16,2560]{1,0:T(8,128)(2,1)S(1)}, bf16[16,2560]{1,0:T(8,128)(2,1)S(1)}, u32[]{:S(2)}, u32[]{:S(2)}) collective-permute-start(bf16[16,2560]{1,0:T(8,128)(2,1)S(1)} %get-tuple-element.49), channel_id=1, source_target_pairs={{8,16},{16,24},{24,0},{0,8},{9,17},{17,25},{25,1},{1,9},{10,18},{1... | collective-permute-start | bytes 245768 | tf_op jit(solution)/shard_map/ppermute | solution.py:318
  38.0 9.9 %collective-permute-start.13 = (bf16[16,2560]{1,0:T(8,128)(2,1)S(1)}, bf16[16,2560]{1,0:T(8,128)(2,1)S(1)}, u32[]{:S(2)}, u32[]{:S(2)}) collective-permute-start(bf16[16,2560]{1,0:T(8,128)(2,1)S(1)} %get-tuple-element.55), channel_id=1, source_target_pairs={{8,16},{16,24},{24,0},{0,8},{9,17},{17,25},{25,1},{1,9},{10,18},{1... | collective-permute-start | bytes 245768 | tf_op jit(solution)/shard_map/ppermute | solution.py:318
  40.6 11.3 %collective-permute-start.16 = (bf16[16,2560]{1,0:T(8,128)(2,1)S(1)}, bf16[16,2560]{1,0:T(8,128)(2,1)S(1)}, u32[]{:S(2)}, u32[]{:S(2)}) collective-permute-start(bf16[16,2560]{1,0:T(8,128)(2,1)S(1)} %get-tuple-element.61), channel_id=1, source_target_pairs={{8,16},{16,24},{24,0},{0,8},{9,17},{17,25},{25,1},{1,9},{10,18},{1... | collective-permute-start | bytes 245768 | tf_op jit(solution)/shard_map/ppermute | solution.py:318
  46.8 6.8 %collective-permute-start.7 = (bf16[16,2560]{1,0:T(8,128)(2,1)S(1)}, bf16[16,2560]{1,0:T(8,128)(2,1)S(1)}, u32[]{:S(2)}, u32[]{:S(2)}) collective-permute-start(bf16[16,2560]{1,0:T(8,128)(2,1)S(1)} %get-tuple-element.43), channel_id=1, source_target_pairs={{8,16},{16,24},{24,0},{0,8},{9,17},{17,25},{25,1},{1,9},{10,18},{1... | collective-permute-start | bytes 245768 | tf_op jit(solution)/shard_map/ppermute | solution.py:318
  46.9 8.3 %collective-permute-start.11 = (bf16[16,2560]{1,0:T(8,128)(2,1)S(1)}, bf16[16,2560]{1,0:T(8,128)(2,1)S(1)}, u32[]{:S(2)}, u32[]{:S(2)}) collective-permute-start(bf16[16,2560]{1,0:T(8,128)(2,1)S(1)} %get-tuple-element.51), channel_id=1, source_target_pairs={{16,24},{24,8},{8,0},{0,16},{17,25},{25,9},{9,1},{1,17},{18,26},{2... | collective-permute-start | bytes 245768 | tf_op jit(solution)/shard_map/ppermute | solution.py:318
  48.0 7.2 %collective-permute-start.14 = (bf16[16,2560]{1,0:T(8,128)(2,1)S(1)}, bf16[16,2560]{1,0:T(8,128)(2,1)S(1)}, u32[]{:S(2)}, u32[]{:S(2)}) collective-permute-start(bf16[16,2560]{1,0:T(8,128)(2,1)S(1)} %get-tuple-element.57), channel_id=1, source_target_pairs={{16,24},{24,8},{8,0},{0,16},{17,25},{25,9},{9,1},{1,17},{18,26},{2... | collective-permute-start | bytes 245768 | tf_op jit(solution)/shard_map/ppermute | solution.py:318
  51.9 4.7 %collective-permute-start.17 = (bf16[16,2560]{1,0:T(8,128)(2,1)S(1)}, bf16[16,2560]{1,0:T(8,128)(2,1)S(1)}, u32[]{:S(2)}, u32[]{:S(2)}) collective-permute-start(bf16[16,2560]{1,0:T(8,128)(2,1)S(1)} %get-tuple-element.63), channel_id=1, source_target_pairs={{16,24},{24,8},{8,0},{0,16},{17,25},{25,9},{9,1},{1,17},{18,26},{2... | collective-permute-start | bytes 245768 | tf_op jit(solution)/shard_map/ppermute | solution.py:318
  53.7 4.5 %collective-permute-start.8 = (bf16[16,2560]{1,0:T(8,128)(2,1)S(1)}, bf16[16,2560]{1,0:T(8,128)(2,1)S(1)}, u32[]{:S(2)}, u32[]{:S(2)}) collective-permute-start(bf16[16,2560]{1,0:T(8,128)(2,1)S(1)} %get-tuple-element.45), channel_id=1, source_target_pairs={{16,24},{24,8},{8,0},{0,16},{17,25},{25,9},{9,1},{1,17},{18,26},{2... | collective-permute-start | bytes 245768 | tf_op jit(solution)/shard_map/ppermute | solution.py:318

commit v4 on v3

--- a/solution.py
+++ b/solution.py
@@ -113,19 +113,19 @@
     def weigh(tops):
         weights = [jnp.exp2((s - top) * SCALE) for s, top in zip(scores, tops)]
         totals = [jnp.sum(w, axis=0, keepdims=True) for w in weights]
-        mixed = [
-            lax.dot_general(
-                w.astype(jnp.bfloat16),
-                jnp.concatenate([t[1, :, g] for t in tile_refs], axis=0),
-                (((0,), (0,)), ((), ())),
-                preferred_element_type=jnp.float32,
-            )
-            for g, w in zip(groups, weights)
-        ]
-        blocks = [
-            [m[b * count : (b + 1) * count, b * HD : (b + 1) * HD] for b in range(heads)]
-            for m, heads in zip(mixed, sizes)
-        ]
+        blocks = []
+        for g, heads, w in zip(groups, sizes, weights):
+            by_query = jnp.transpose(w.astype(jnp.bfloat16))
+            parts = []
+            for b in range(0, heads, 2):
+                pair = slice(g.start + b * HD, g.start + (b + 2) * HD)
+                both = jnp.dot(
+                    by_query[b * count : (b + 2) * count],
+                    jnp.concatenate([t[1, :, pair] for t in tile_refs], axis=0),
+                    preferred_element_type=jnp.float32,
+                )
+                parts += [both[:count, :HD], both[count:, HD:]]
+            blocks.append(parts)
         return totals, blocks
 
     return states, tops, weigh

time: 59.1 us -> 58.8 us (level)
  starting transfers between devices: 22.1 us -> 21.3 us
    ppermute x12, starting transfers between devices: 16.1 us -> 15.3 us  [on_device(): source = lax.ppermute(following[p], 'section', hop)]
where the time goes in v4:
time: 58.8 us; the launch traced here: 58.6 us
  waiting for transfers between devices  30.4 us (52%)
  starting transfers between devices  21.3 us (36%)
  Pallas kernels  5.62 us (10%)
  local copies, waits for them, and re-layouts  1.1 us (2%)
    ppermute x6, waiting for transfers between devices, move(): return lax.ppermute(tile, ('section', 'tile'), on_all(pairs))  18.9 us
    ppermute x12, starting transfers between devices, on_device(): source = lax.ppermute(following[p], 'section', hop)  15.3 us
    ppermute x12, waiting for transfers between devices, on_device(): source = lax.ppermute(following[p], 'section', hop)  11.5 us
    ppermute x6, starting transfers between devices, move(): return lax.ppermute(tile, ('section', 'tile'), on_all(pairs))  6.07 us
    pallas_call x3, Pallas kernels, partial_attend(): pl.pallas_call(functools.partial(partial_body, slots, bool(carry), last),...  2.87 us
    pallas_call x3, Pallas kernels, split_keys_values(): pl.pallas_call(split_body, out_shape=jax.ShapeDtypeStruct((2, rows, chann...  1.33 us
  transfers between devices with their start and end apart: 18, of which 8 were waited for; matrix products, arithmetic and copies ran while one was open for 0% of the time, Pallas kernels for 5%

profile of v4, /device:TPU:0, one launch (start us, length us, event | category | flops | bytes accessed | tf_op | source)
XLA Modules:
  0.0 58.6 jit_solution(16093762310466851201)
XLA Ops:
  0.0 0.5 collective-permute-start
  0.5 1.1 %copy-done.2 = bf16[1,64,2,2560]{3,2,1,0:T(2,128)(2,1)S(1)} copy-done((bf16[1,64,2,2560]{3,2,1,0:T(2,128)(2,1)S(1)}, bf16[1,64,2,2560]{3,2,1,0:T(2,128)(2,1)}, u32[]{:S(2)}) %copy-start.2) | copy-done | bytes 655384
  1.6 0.4 split_kv.5.refs_0_
  2.0 0.0 copy-start.3
  2.0 2.6 %collective-permute-start.2 = (bf16[2,64,2560]{2,1,0:T(8,128)(2,1)S(1)}, bf16[2,64,2560]{2,1,0:T(8,128)(2,1)S(1)}, u32[]{:S(2)}, u32[]{:S(2)}) collective-permute-start(bf16[2,64,2560]{2,1,0:T(8,128)(2,1)S(1)} %split_kv.5.refs_0_), channel_id=1, source_target_pairs={{1,0},{6,7},{3,1},{5,3},{7,5},{0,2},{2,4},{4,6},{9,8},{14,15},{11,... | collective-permute-start | bytes 1966088 | tf_op jit(solution)/shard_map/ppermute | solution.py:275
  4.7 0.0 collective-permute-start.5
  4.7 12.2 %collective-permute-done.kv_ref = bf16[64,2,2560]{2,1,0:T(2,128)(2,1)S(1)} collective-permute-done((bf16[64,2,2560]{2,1,0:T(2,128)(2,1)}, bf16[64,2,2560]{2,1,0:T(2,128)(2,1)S(1)}, u32[]{:S(2)}, u32[]{:S(2)}) %collective-permute-start) | collective-permute-done | bytes 655392 | tf_op jit(solution)/shard_map/ppermute | solution.py:275
  16.9 0.4 split_kv.4.refs_0_.refs_1_
  17.3 0.0 copy-start.1
  17.3 2.5 %collective-permute-start.1 = (bf16[64,2,2560]{2,1,0:T(2,128)(2,1)S(1)}, bf16[64,2,2560]{2,1,0:T(2,128)(2,1)S(1)}, u32[]{:S(2)}, u32[]{:S(2)}) collective-permute-start(bf16[64,2,2560]{2,1,0:T(2,128)(2,1)S(1)} %collective-permute-done.kv_ref), channel_id=1, source_target_pairs={{0,8},{7,15},{1,2},{3,4},{5,6},{2,1},{4,3},{6,5},{8,0},{15,7},{9,1... | collective-permute-start | bytes 1966088 | tf_op jit(solution)/shard_map/ppermute | solution.py:275
  19.8 0.0 collective-permute-done.2.refs_1_.refs_2_
  19.8 0.2 collective-permute-start.4
  20.0 0.3 collective-permute-start.3
  20.3 0.6 mask_bias.1.bias_ref
  20.9 0.0 collective-permute-done.5.refs_1_.refs_4_
  20.9 0.0 copy-done
  20.9 0.8 %partial_attend.3 = (f32[10,128]{1,0:T(8,128)S(1)}, f32[10,128]{1,0:T(8,128)S(1)}, f32[64,2560]{1,0:T(8,128)S(1)}) custom-call(f32[448,128]{1,0:T(8,128)S(1)} %mask_bias.1.bias_ref, bf16[64,2560]{1,0:T(8,128)(2,1)S(1)} %copy-done, f32[1,2560]{1,0:T(1,128)S(1)} %copy-done.1, bf16[2,64,2560]{2,1,0:T(8,128)(2,1)S(1)} %split_kv.5.refs_0_, ...), custom_call_target="tpu_custom_call" | custom-call | flops 83886080 | bytes 2293760 | tf_op jit(solution)/shard_map/partial_attend/pallas_call | solution.py:205
  21.7 6.7 %collective-permute-done.1.kv_ref = bf16[64,2,2560]{2,1,0:T(2,128)(2,1)S(1)} collective-permute-done((bf16[64,2,2560]{2,1,0:T(2,128)(2,1)S(1)}, bf16[64,2,2560]{2,1,0:T(2,128)(2,1)S(1)}, u32[]{:S(2)}, u32[]{:S(2)}) %collective-permute-start.1) | collective-permute-done | bytes 655392 | tf_op jit(solution)/shard_map/ppermute | solution.py:275
  28.3 0.4 split_kv.3.refs_0_.refs_3_
  28.8 0.0 collective-permute-done.4.refs_3_.refs_6_
  28.8 0.0 collective-permute-done.3.refs_2_.refs_5_
  28.8 1.1 %partial_attend.4 = (f32[10,128]{1,0:T(8,128)S(1)}, f32[10,128]{1,0:T(8,128)S(1)}, f32[64,2560]{1,0:T(8,128)S(1)}) custom-call(f32[448,128]{1,0:T(8,128)S(1)} %mask_bias.1.bias_ref, bf16[64,2560]{1,0:T(8,128)(2,1)S(1)} %copy-done, f32[1,2560]{1,0:T(1,128)S(1)} %copy-done.1, bf16[2,64,2560]{2,1,0:T(8,128)(2,1)S(1)} %split_kv.4.refs_0_.refs_1_, ...), custom_call_target="tpu_custom_call" | custom-call | flops 167772160 | bytes 3604480 | tf_op jit(solution)/shard_map/partial_attend/pallas_call | solution.py:205
  29.9 1.0 %partial_attend.5 = (bf16[16,2560]{1,0:T(8,128)(2,1)S(1)}, bf16[16,2560]{1,0:T(8,128)(2,1)S(1)}, bf16[16,2560]{1,0:T(8,128)(2,1)S(1)}, bf16[16,2560]{1,0:T(8,128...) custom-call(f32[448,128]{1,0:T(8,128)S(1)} %mask_bias.1.bias_ref, ...), custom_call_target="tpu_custom_call" | custom-call | flops 41943040 | bytes 1638400 | tf_op jit(solution)/shard_map/partial_attend/pallas_call | solution.py:205
  30.9 0.1 collective-permute-start.9
  31.0 1.5 %collective-permute-start.12 = (bf16[16,2560]{1,0:T(8,128)(2,1)S(1)}, bf16[16,2560]{1,0:T(8,128)(2,1)S(1)}, u32[]{:S(2)}, u32[]{:S(2)}) collective-permute-start(bf16[16,2560]{1,0:T(8,128)(2,1)S(1)} %get-tuple-element.53), channel_id=1, source_target_pairs={{0,8},{8,24},{24,16},{16,0},{1,9},{9,25},{25,17},{17,1},{2,10},{10... | collective-permute-start | bytes 245768 | tf_op jit(solution)/shard_map/ppermute | solution.py:318
  32.4 0.5 collective-permute-start.15
  33.0 2.0 %collective-permute-start.6 = (bf16[16,2560]{1,0:T(8,128)(2,1)S(1)}, bf16[16,2560]{1,0:T(8,128)(2,1)S(1)}, u32[]{:S(2)}, u32[]{:S(2)}) collective-permute-start(bf16[16,2560]{1,0:T(8,128)(2,1)S(1)} %get-tuple-element.41), channel_id=1, source_target_pairs={{0,8},{8,24},{24,16},{16,0},{1,9},{9,25},{25,17},{17,1},{2,10},{10... | collective-permute-start | bytes 245768 | tf_op jit(solution)/shard_map/ppermute | solution.py:318
  35.0 1.3 %collective-permute-done.9.src_ref = bf16[16,2560]{1,0:T(8,128)(2,1)S(1)} collective-permute-done((bf16[16,2560]{1,0:T(8,128)(2,1)S(1)}, bf16[16,2560]{1,0:T(8,128)(2,1)S(1)}, u32[]{:S(2)}, u32[]{:S(2)}) %collective-permute-start.9) | collective-permute-done | bytes 81952 | tf_op jit(solution)/shard_map/ppermute | solution.py:318
  36.3 1.4 %collective-permute-start.10 = (bf16[16,2560]{1,0:T(8,128)(2,1)S(1)}, bf16[16,2560]{1,0:T(8,128)(2,1)S(1)}, u32[]{:S(2)}, u32[]{:S(2)}) collective-permute-start(bf16[16,2560]{1,0:T(8,128)(2,1)S(1)} %get-tuple-element.49), channel_id=1, source_target_pairs={{8,16},{16,24},{24,0},{0,8},{9,17},{17,25},{25,1},{1,9},{10,18},{1... | collective-permute-start | bytes 245768 | tf_op jit(solution)/shard_map/ppermute | solution.py:318
  37.7 0.4 collective-permute-done.12.src_ref
  38.0 1.4 %collective-permute-start.13 = (bf16[16,2560]{1,0:T(8,128)(2,1)S(1)}, bf16[16,2560]{1,0:T(8,128)(2,1)S(1)}, u32[]{:S(2)}, u32[]{:S(2)}) collective-permute-start(bf16[16,2560]{1,0:T(8,128)(2,1)S(1)} %get-tuple-element.55), channel_id=1, source_target_pairs={{8,16},{16,24},{24,0},{0,8},{9,17},{17,25},{25,1},{1,9},{10,18},{1... | collective-permute-start | bytes 245768 | tf_op jit(solution)/shard_map/ppermute | solution.py:318
  39.4 1.2 %collective-permute-done.15.src_ref = bf16[16,2560]{1,0:T(8,128)(2,1)S(1)} collective-permute-done((bf16[16,2560]{1,0:T(8,128)(2,1)S(1)}, bf16[16,2560]{1,0:T(8,128)(2,1)S(1)}, u32[]{:S(2)}, u32[]{:S(2)}) %collective-permute-start.15) | collective-permute-done | bytes 81952 | tf_op jit(solution)/shard_map/ppermute | solution.py:318
  40.6 0.6 collective-permute-start.16
  41.2 5.7 %collective-permute-done.6.src_ref = bf16[16,2560]{1,0:T(8,128)(2,1)S(1)} collective-permute-done((bf16[16,2560]{1,0:T(8,128)(2,1)S(1)}, bf16[16,2560]{1,0:T(8,128)(2,1)S(1)}, u32[]{:S(2)}, u32[]{:S(2)}) %collective-permute-start.6) | collective-permute-done | bytes 81952 | tf_op jit(solution)/shard_map/ppermute | solution.py:318
  46.8 0.0 collective-permute-start.7
  46.9 0.0 collective-permute-done.10.src_ref
  46.9 0.9 %collective-permute-start.11 = (bf16[16,2560]{1,0:T(8,128)(2,1)S(1)}, bf16[16,2560]{1,0:T(8,128)(2,1)S(1)}, u32[]{:S(2)}, u32[]{:S(2)}) collective-permute-start(bf16[16,2560]{1,0:T(8,128)(2,1)S(1)} %get-tuple-element.51), channel_id=1, source_target_pairs={{16,24},{24,8},{8,0},{0,16},{17,25},{25,9},{9,1},{1,17},{18,26},{2... | collective-permute-start | bytes 245768 | tf_op jit(solution)/shard_map/ppermute | solution.py:318
  47.8 0.0 collective-permute-done.13.src_ref
  47.8 3.9 %collective-permute-start.14 = (bf16[16,2560]{1,0:T(8,128)(2,1)S(1)}, bf16[16,2560]{1,0:T(8,128)(2,1)S(1)}, u32[]{:S(2)}, u32[]{:S(2)}) collective-permute-start(bf16[16,2560]{1,0:T(8,128)(2,1)S(1)} %get-tuple-element.57), channel_id=1, source_target_pairs={{16,24},{24,8},{8,0},{0,16},{17,25},{25,9},{9,1},{1,17},{18,26},{2... | collective-permute-start | bytes 245768 | tf_op jit(solution)/shard_map/ppermute | solution.py:318
  51.8 0.0 collective-permute-done.16.src_ref
  51.8 1.4 %collective-permute-start.17 = (bf16[16,2560]{1,0:T(8,128)(2,1)S(1)}, bf16[16,2560]{1,0:T(8,128)(2,1)S(1)}, u32[]{:S(2)}, u32[]{:S(2)}) collective-permute-start(bf16[16,2560]{1,0:T(8,128)(2,1)S(1)} %get-tuple-element.63), channel_id=1, source_target_pairs={{16,24},{24,8},{8,0},{0,16},{17,25},{25,9},{9,1},{1,17},{18,26},{2... | collective-permute-start | bytes 245768 | tf_op jit(solution)/shard_map/ppermute | solution.py:318
  53.2 0.0 collective-permute-done.7.src_ref
  53.2 1.6 %collective-permute-start.8 = (bf16[16,2560]{1,0:T(8,128)(2,1)S(1)}, bf16[16,2560]{1,0:T(8,128)(2,1)S(1)}, u32[]{:S(2)}, u32[]{:S(2)}) collective-permute-start(bf16[16,2560]{1,0:T(8,128)(2,1)S(1)} %get-tuple-element.45), channel_id=1, source_target_pairs={{16,24},{24,8},{8,0},{0,16},{17,25},{25,9},{9,1},{1,17},{18,26},{2... | collective-permute-start | bytes 245768 | tf_op jit(solution)/shard_map/ppermute | solution.py:318
  54.8 0.0 collective-permute-done.11.src_ref
  54.8 0.0 collective-permute-done.14.src_ref
  54.9 1.4 %collective-permute-done.17.src_ref = bf16[16,2560]{1,0:T(8,128)(2,1)S(1)} collective-permute-done((bf16[16,2560]{1,0:T(8,128)(2,1)S(1)}, bf16[16,2560]{1,0:T(8,128)(2,1)S(1)}, u32[]{:S(2)}, u32[]{:S(2)}) %collective-permute-start.17) | collective-permute-done | bytes 81952 | tf_op jit(solution)/shard_map/ppermute | solution.py:318
  56.3 1.6 %collective-permute-done.8.src_ref = bf16[16,2560]{1,0:T(8,128)(2,1)S(1)} collective-permute-done((bf16[16,2560]{1,0:T(8,128)(2,1)S(1)}, bf16[16,2560]{1,0:T(8,128)(2,1)S(1)}, u32[]{:S(2)}, u32[]{:S(2)}) %collective-permute-start.8) | collective-permute-done | bytes 81952 | tf_op jit(solution)/shard_map/ppermute | solution.py:318
  57.9 0.7 %attend.23 = bf16[64,2560]{1,0:T(8,128)(2,1)} custom-call(f32[448,128]{1,0:T(8,128)S(1)} %mask_bias.1.bias_ref, bf16[16,2560]{1,0:T(8,128)(2,1)S(1)} %collective-permute-done.8.src_ref, f32[1,2560]{1,0:T(1,128)S(1)} %copy-done.1, bf16[2,64,2560]{2,1,0:T(8,128)(2,1)S(1)} %split_kv.5.refs_0_, bf16[2,64,2560]{2,1,0:T(8,128)(2,1)S(1)} %split_kv.4.refs_0_.refs_1_, ...), custom_call_target="tpu_custom_call" | custom-call | flops 73400320 | bytes 4833280 | tf_op jit(solution)/shard_map/attend/pallas_call | solution.py:255
  (15 shorter events, 0.1 us)
Async XLA Ops:
  0.0 16.9 %collective-permute-start = (bf16[64,2,2560]{2,1,0:T(2,128)(2,1)}, bf16[64,2,2560]{2,1,0:T(2,128)(2,1)S(1)}, u32[]{:S(2)}, u32[]{:S(2)}) collective-permute-start(bf16[64,2,2560]{2,1,0:T(2,128)(2,1)} %bitcast.2), channel_id=1, source_target_pairs={{0,1},{7,6},{1,3},{3,5},{5,7},{2,0},{4,2},{6,4},{8,9},{15,14},{9,1... | collective-permute-start | bytes 1966088 | tf_op jit(solution)/shard_map/ppermute | solution.py:275
  0.5 1.1 %copy-start.2 = (bf16[1,64,2,2560]{3,2,1,0:T(2,128)(2,1)S(1)}, bf16[1,64,2,2560]{3,2,1,0:T(2,128)(2,1)}, u32[]{:S(2)}) copy-start(bf16[1,64,2,2560]{3,2,1,0:T(2,128)(2,1)} %param.5) | copy-start | bytes 1966084
  2.0 18.3 %copy-start.3 = (s32[1,7]{1,0:T(1,128)S(1)}, s32[1,7]{1,0:T(1,128)}, u32[]{:S(2)}) copy-start(s32[1,7]{1,0:T(1,128)} %mask_ref.1) | copy-start | bytes 88
  2.0 17.7 %collective-permute-start.2 = (bf16[2,64,2560]{2,1,0:T(8,128)(2,1)S(1)}, bf16[2,64,2560]{2,1,0:T(8,128)(2,1)S(1)}, u32[]{:S(2)}, u32[]{:S(2)}) collective-permute-start(bf16[2,64,2560]{2,1,0:T(8,128)(2,1)S(1)} %split_kv.5.refs_0_), channel_id=1, source_target_pairs={{1,0},{6,7},{3,1},{5,3},{7,5},{0,2},{2,4},{4,6},{9,8},{14,15},{11,... | collective-permute-start | bytes 1966088 | tf_op jit(solution)/shard_map/ppermute | solution.py:275
  4.7 16.2 %collective-permute-start.5 = (bf16[2,64,2560]{2,1,0:T(8,128)(2,1)S(1)}, bf16[2,64,2560]{2,1,0:T(8,128)(2,1)S(1)}, u32[]{:S(2)}, u32[]{:S(2)}) collective-permute-start(bf16[2,64,2560]{2,1,0:T(8,128)(2,1)S(1)} %split_kv.5.refs_0_), channel_id=1, source_target_pairs={{0,1},{1,0},{2,3},{3,2},{4,5},{5,4},{6,7},{7,6},{8,9},{9,8},{10,11... | collective-permute-start | bytes 1966088 | tf_op jit(solution)/shard_map/ppermute | solution.py:275
  16.9 4.0 %copy-start = (bf16[64,2560]{1,0:T(8,128)(2,1)S(1)}, bf16[64,2560]{1,0:T(8,128)(2,1)}, u32[]{:S(2)}) copy-start(bf16[64,2560]{1,0:T(8,128)(2,1)} %src_ref.5) | copy-start | bytes 983044
  17.3 3.6 %copy-start.1 = (f32[1,2560]{1,0:T(1,128)S(1)}, f32[1,2560]{1,0:T(1,128)}, u32[]{:S(2)}) copy-start(f32[1,2560]{1,0:T(1,128)} %gain_ref.29) | copy-start | bytes 30724
  17.3 11.0 %collective-permute-start.1 = (bf16[64,2,2560]{2,1,0:T(2,128)(2,1)S(1)}, bf16[64,2,2560]{2,1,0:T(2,128)(2,1)S(1)}, u32[]{:S(2)}, u32[]{:S(2)}) collective-permute-start(bf16[64,2,2560]{2,1,0:T(2,128)(2,1)S(1)} %collective-permute-done.kv_ref), channel_id=1, source_target_pairs={{0,8},{7,15},{1,2},{3,4},{5,6},{2,1},{4,3},{6,5},{8,0},{15,7},{9,1... | collective-permute-start | bytes 1966088 | tf_op jit(solution)/shard_map/ppermute | solution.py:275
  19.8 9.0 %collective-permute-start.4 = (bf16[2,64,2560]{2,1,0:T(8,128)(2,1)S(1)}, bf16[2,64,2560]{2,1,0:T(8,128)(2,1)S(1)}, u32[]{:S(2)}, u32[]{:S(2)}) collective-permute-start(bf16[2,64,2560]{2,1,0:T(8,128)(2,1)S(1)} %collective-permute-done.2.refs_1_.refs_2_), channel_id=1, source_target_pairs={{0,1},{1,0},{2,3},{3,2},{4,5},{5,4},{6,7},{7,6},{8,9},{9,8},{10,11... | collective-permute-start | bytes 1966088 | tf_op jit(solution)/shard_map/ppermute | solution.py:275
  20.0 8.8 %collective-permute-start.3 = (bf16[2,64,2560]{2,1,0:T(8,128)(2,1)S(1)}, bf16[2,64,2560]{2,1,0:T(8,128)(2,1)S(1)}, u32[]{:S(2)}, u32[]{:S(2)}) collective-permute-start(bf16[2,64,2560]{2,1,0:T(8,128)(2,1)S(1)} %split_kv.4.refs_0_.refs_1_), channel_id=1, source_target_pairs={{0,1},{1,0},{2,3},{3,2},{4,5},{5,4},{6,7},{7,6},{8,9},{9,8},{10,11... | collective-permute-start | bytes 1966088 | tf_op jit(solution)/shard_map/ppermute | solution.py:275
  30.9 5.4 %collective-permute-start.9 = (bf16[16,2560]{1,0:T(8,128)(2,1)S(1)}, bf16[16,2560]{1,0:T(8,128)(2,1)S(1)}, u32[]{:S(2)}, u32[]{:S(2)}) collective-permute-start(bf16[16,2560]{1,0:T(8,128)(2,1)S(1)} %get-tuple-element.47), channel_id=1, source_target_pairs={{0,8},{8,24},{24,16},{16,0},{1,9},{9,25},{25,17},{17,1},{2,10},{10... | collective-permute-start | bytes 245768 | tf_op jit(solution)/shard_map/ppermute | solution.py:318
  31.0 7.1 %collective-permute-start.12 = (bf16[16,2560]{1,0:T(8,128)(2,1)S(1)}, bf16[16,2560]{1,0:T(8,128)(2,1)S(1)}, u32[]{:S(2)}, u32[]{:S(2)}) collective-permute-start(bf16[16,2560]{1,0:T(8,128)(2,1)S(1)} %get-tuple-element.53), channel_id=1, source_target_pairs={{0,8},{8,24},{24,16},{16,0},{1,9},{9,25},{25,17},{17,1},{2,10},{10... | collective-permute-start | bytes 245768 | tf_op jit(solution)/shard_map/ppermute | solution.py:318
  32.4 8.2 %collective-permute-start.15 = (bf16[16,2560]{1,0:T(8,128)(2,1)S(1)}, bf16[16,2560]{1,0:T(8,128)(2,1)S(1)}, u32[]{:S(2)}, u32[]{:S(2)}) collective-permute-start(bf16[16,2560]{1,0:T(8,128)(2,1)S(1)} %get-tuple-element.59), channel_id=1, source_target_pairs={{0,8},{8,24},{24,16},{16,0},{1,9},{9,25},{25,17},{17,1},{2,10},{10... | collective-permute-start | bytes 245768 | tf_op jit(solution)/shard_map/ppermute | solution.py:318
  33.0 13.9 %collective-permute-start.6 = (bf16[16,2560]{1,0:T(8,128)(2,1)S(1)}, bf16[16,2560]{1,0:T(8,128)(2,1)S(1)}, u32[]{:S(2)}, u32[]{:S(2)}) collective-permute-start(bf16[16,2560]{1,0:T(8,128)(2,1)S(1)} %get-tuple-element.41), channel_id=1, source_target_pairs={{0,8},{8,24},{24,16},{16,0},{1,9},{9,25},{25,17},{17,1},{2,10},{10... | collective-permute-start | bytes 245768 | tf_op jit(solution)/shard_map/ppermute | solution.py:318
  36.3 10.6 %collective-permute-start.10 = (bf16[16,2560]{1,0:T(8,128)(2,1)S(1)}, bf16[16,2560]{1,0:T(8,128)(2,1)S(1)}, u32[]{:S(2)}, u32[]{:S(2)}) collective-permute-start(bf16[16,2560]{1,0:T(8,128)(2,1)S(1)} %get-tuple-element.49), channel_id=1, source_target_pairs={{8,16},{16,24},{24,0},{0,8},{9,17},{17,25},{25,1},{1,9},{10,18},{1... | collective-permute-start | bytes 245768 | tf_op jit(solution)/shard_map/ppermute | solution.py:318
  38.0 9.8 %collective-permute-start.13 = (bf16[16,2560]{1,0:T(8,128)(2,1)S(1)}, bf16[16,2560]{1,0:T(8,128)(2,1)S(1)}, u32[]{:S(2)}, u32[]{:S(2)}) collective-permute-start(bf16[16,2560]{1,0:T(8,128)(2,1)S(1)} %get-tuple-element.55), channel_id=1, source_target_pairs={{8,16},{16,24},{24,0},{0,8},{9,17},{17,25},{25,1},{1,9},{10,18},{1... | collective-permute-start | bytes 245768 | tf_op jit(solution)/shard_map/ppermute | solution.py:318
  40.6 11.2 %collective-permute-start.16 = (bf16[16,2560]{1,0:T(8,128)(2,1)S(1)}, bf16[16,2560]{1,0:T(8,128)(2,1)S(1)}, u32[]{:S(2)}, u32[]{:S(2)}) collective-permute-start(bf16[16,2560]{1,0:T(8,128)(2,1)S(1)} %get-tuple-element.61), channel_id=1, source_target_pairs={{8,16},{16,24},{24,0},{0,8},{9,17},{17,25},{25,1},{1,9},{10,18},{1... | collective-permute-start | bytes 245768 | tf_op jit(solution)/shard_map/ppermute | solution.py:318
  46.8 6.4 %collective-permute-start.7 = (bf16[16,2560]{1,0:T(8,128)(2,1)S(1)}, bf16[16,2560]{1,0:T(8,128)(2,1)S(1)}, u32[]{:S(2)}, u32[]{:S(2)}) collective-permute-start(bf16[16,2560]{1,0:T(8,128)(2,1)S(1)} %get-tuple-element.43), channel_id=1, source_target_pairs={{8,16},{16,24},{24,0},{0,8},{9,17},{17,25},{25,1},{1,9},{10,18},{1... | collective-permute-start | bytes 245768 | tf_op jit(solution)/shard_map/ppermute | solution.py:318
  46.9 7.9 %collective-permute-start.11 = (bf16[16,2560]{1,0:T(8,128)(2,1)S(1)}, bf16[16,2560]{1,0:T(8,128)(2,1)S(1)}, u32[]{:S(2)}, u32[]{:S(2)}) collective-permute-start(bf16[16,2560]{1,0:T(8,128)(2,1)S(1)} %get-tuple-element.51), channel_id=1, source_target_pairs={{16,24},{24,8},{8,0},{0,16},{17,25},{25,9},{9,1},{1,17},{18,26},{2... | collective-permute-start | bytes 245768 | tf_op jit(solution)/shard_map/ppermute | solution.py:318
  47.8 7.0 %collective-permute-start.14 = (bf16[16,2560]{1,0:T(8,128)(2,1)S(1)}, bf16[16,2560]{1,0:T(8,128)(2,1)S(1)}, u32[]{:S(2)}, u32[]{:S(2)}) collective-permute-start(bf16[16,2560]{1,0:T(8,128)(2,1)S(1)} %get-tuple-element.57), channel_id=1, source_target_pairs={{16,24},{24,8},{8,0},{0,16},{17,25},{25,9},{9,1},{1,17},{18,26},{2... | collective-permute-start | bytes 245768 | tf_op jit(solution)/shard_map/ppermute | solution.py:318
  51.8 4.5 %collective-permute-start.17 = (bf16[16,2560]{1,0:T(8,128)(2,1)S(1)}, bf16[16,2560]{1,0:T(8,128)(2,1)S(1)}, u32[]{:S(2)}, u32[]{:S(2)}) collective-permute-start(bf16[16,2560]{1,0:T(8,128)(2,1)S(1)} %get-tuple-element.63), channel_id=1, source_target_pairs={{16,24},{24,8},{8,0},{0,16},{17,25},{25,9},{9,1},{1,17},{18,26},{2... | collective-permute-start | bytes 245768 | tf_op jit(solution)/shard_map/ppermute | solution.py:318
  53.2 4.7 %collective-permute-start.8 = (bf16[16,2560]{1,0:T(8,128)(2,1)S(1)}, bf16[16,2560]{1,0:T(8,128)(2,1)S(1)}, u32[]{:S(2)}, u32[]{:S(2)}) collective-permute-start(bf16[16,2560]{1,0:T(8,128)(2,1)S(1)} %get-tuple-element.45), channel_id=1, source_target_pairs={{16,24},{24,8},{8,0},{0,16},{17,25},{25,9},{9,1},{1,17},{18,26},{2... | collective-permute-start | bytes 245768 | tf_op jit(solution)/shard_map/ppermute | solution.py:318

commit v5 on v4

--- a/solution.py
+++ b/solution.py
@@ -138,8 +138,8 @@
     totals, mixed = weigh(tops)
     done = []
     for g, heads, state, blocks, total in zip(groups, sizes, states, mixed, totals):
-        by_row = per_row(total, heads, count)
-        parts = [m / by_row[b * count : (b + 1) * count] for b, m in enumerate(blocks)]
+        by_row = per_row(1.0 / total, heads, count)
+        parts = [m * by_row[b * count : (b + 1) * count] for b, m in enumerate(blocks)]
         done.append((g, state, jnp.concatenate(parts, axis=1).astype(jnp.bfloat16)))
     return done
 
@@ -181,8 +181,8 @@
                 for b, m in enumerate(blocks):
                     sum_out[:, g.start + b * HD : g.start + (b + 1) * HD] = m
                 continue
-            by_row = per_row(total, heads, rows)
-            parts = [m / by_row[b * rows : (b + 1) * rows] for b, m in enumerate(blocks)]
+            by_row = per_row(1.0 / total, heads, rows)
+            parts = [m * by_row[b * rows : (b + 1) * rows] for b, m in enumerate(blocks)]
             result = jnp.concatenate(parts, axis=1).astype(jnp.bfloat16)
             state = (states[n] + result.astype(jnp.float32)).astype(jnp.bfloat16)
             count = rows // PIECES

time: 58.8 us -> 58.6 us (level)
  no operation moved by 1% of the time
where the time goes in v5:
time: 58.6 us; the launch traced here: 58.5 us
  waiting for transfers between devices  30.4 us (52%)
  starting transfers between devices  21.2 us (36%)
  Pallas kernels  5.62 us (10%)
  local copies, waits for them, and re-layouts  1.1 us (2%)
    ppermute x6, waiting for transfers between devices, move(): return lax.ppermute(tile, ('section', 'tile'), on_all(pairs))  18.9 us
    ppermute x12, starting transfers between devices, on_device(): source = lax.ppermute(following[p], 'section', hop)  15.1 us
    ppermute x12, waiting for transfers between devices, on_device(): source = lax.ppermute(following[p], 'section', hop)  11.5 us
    ppermute x6, starting transfers between devices, move(): return lax.ppermute(tile, ('section', 'tile'), on_all(pairs))  6.07 us
    pallas_call x3, Pallas kernels, partial_attend(): pl.pallas_call(functools.partial(partial_body, slots, bool(carry), last),...  2.87 us
    pallas_call x3, Pallas kernels, split_keys_values(): pl.pallas_call(split_body, out_shape=jax.ShapeDtypeStruct((2, rows, chann...  1.33 us
  transfers between devices with their start and end apart: 18, of which 8 were waited for; matrix products, arithmetic and copies ran while one was open for 0% of the time, Pallas kernels for 5%

profile of v5, /device:TPU:0, one launch (start us, length us, event | category | flops | bytes accessed | tf_op | source)
XLA Modules:
  0.0 58.5 jit_solution(9104253593892349090)
XLA Ops:
  0.0 0.5 collective-permute-start
  0.5 1.1 %copy-done.2 = bf16[1,64,2,2560]{3,2,1,0:T(2,128)(2,1)S(1)} copy-done((bf16[1,64,2,2560]{3,2,1,0:T(2,128)(2,1)S(1)}, bf16[1,64,2,2560]{3,2,1,0:T(2,128)(2,1)}, u32[]{:S(2)}) %copy-start.2) | copy-done | bytes 655384
  1.6 0.4 split_kv.5.refs_0_
  2.0 0.0 copy-start.3
  2.0 2.6 %collective-permute-start.2 = (bf16[2,64,2560]{2,1,0:T(8,128)(2,1)S(1)}, bf16[2,64,2560]{2,1,0:T(8,128)(2,1)S(1)}, u32[]{:S(2)}, u32[]{:S(2)}) collective-permute-start(bf16[2,64,2560]{2,1,0:T(8,128)(2,1)S(1)} %split_kv.5.refs_0_), channel_id=1, source_target_pairs={{1,0},{6,7},{3,1},{5,3},{7,5},{0,2},{2,4},{4,6},{9,8},{14,15},{11,... | collective-permute-start | bytes 1966088 | tf_op jit(solution)/shard_map/ppermute | solution.py:275
  4.7 0.0 collective-permute-start.5
  4.7 12.2 %collective-permute-done.kv_ref = bf16[64,2,2560]{2,1,0:T(2,128)(2,1)S(1)} collective-permute-done((bf16[64,2,2560]{2,1,0:T(2,128)(2,1)}, bf16[64,2,2560]{2,1,0:T(2,128)(2,1)S(1)}, u32[]{:S(2)}, u32[]{:S(2)}) %collective-permute-start) | collective-permute-done | bytes 655392 | tf_op jit(solution)/shard_map/ppermute | solution.py:275
  16.9 0.4 split_kv.4.refs_0_.refs_1_
  17.3 0.0 copy-start.1
  17.3 2.5 %collective-permute-start.1 = (bf16[64,2,2560]{2,1,0:T(2,128)(2,1)S(1)}, bf16[64,2,2560]{2,1,0:T(2,128)(2,1)S(1)}, u32[]{:S(2)}, u32[]{:S(2)}) collective-permute-start(bf16[64,2,2560]{2,1,0:T(2,128)(2,1)S(1)} %collective-permute-done.kv_ref), channel_id=1, source_target_pairs={{0,8},{7,15},{1,2},{3,4},{5,6},{2,1},{4,3},{6,5},{8,0},{15,7},{9,1... | collective-permute-start | bytes 1966088 | tf_op jit(solution)/shard_map/ppermute | solution.py:275
  19.8 0.0 collective-permute-done.2.refs_1_.refs_2_
  19.8 0.2 collective-permute-start.4
  20.0 0.3 collective-permute-start.3
  20.3 0.6 mask_bias.1.bias_ref
  20.9 0.0 collective-permute-done.5.refs_1_.refs_4_
  20.9 0.0 copy-done
  20.9 0.8 %partial_attend.3 = (f32[10,128]{1,0:T(8,128)S(1)}, f32[10,128]{1,0:T(8,128)S(1)}, f32[64,2560]{1,0:T(8,128)S(1)}) custom-call(f32[448,128]{1,0:T(8,128)S(1)} %mask_bias.1.bias_ref, bf16[64,2560]{1,0:T(8,128)(2,1)S(1)} %copy-done, f32[1,2560]{1,0:T(1,128)S(1)} %copy-done.1, bf16[2,64,2560]{2,1,0:T(8,128)(2,1)S(1)} %split_kv.5.refs_0_, ...), custom_call_target="tpu_custom_call" | custom-call | flops 83886080 | bytes 2293760 | tf_op jit(solution)/shard_map/partial_attend/pallas_call | solution.py:205
  21.7 6.7 %collective-permute-done.1.kv_ref = bf16[64,2,2560]{2,1,0:T(2,128)(2,1)S(1)} collective-permute-done((bf16[64,2,2560]{2,1,0:T(2,128)(2,1)S(1)}, bf16[64,2,2560]{2,1,0:T(2,128)(2,1)S(1)}, u32[]{:S(2)}, u32[]{:S(2)}) %collective-permute-start.1) | collective-permute-done | bytes 655392 | tf_op jit(solution)/shard_map/ppermute | solution.py:275
  28.3 0.4 split_kv.3.refs_0_.refs_3_
  28.8 0.0 collective-permute-done.4.refs_3_.refs_6_
  28.8 0.0 collective-permute-done.3.refs_2_.refs_5_
  28.8 1.1 %partial_attend.4 = (f32[10,128]{1,0:T(8,128)S(1)}, f32[10,128]{1,0:T(8,128)S(1)}, f32[64,2560]{1,0:T(8,128)S(1)}) custom-call(f32[448,128]{1,0:T(8,128)S(1)} %mask_bias.1.bias_ref, bf16[64,2560]{1,0:T(8,128)(2,1)S(1)} %copy-done, f32[1,2560]{1,0:T(1,128)S(1)} %copy-done.1, bf16[2,64,2560]{2,1,0:T(8,128)(2,1)S(1)} %split_kv.4.refs_0_.refs_1_, ...), custom_call_target="tpu_custom_call" | custom-call | flops 167772160 | bytes 3604480 | tf_op jit(solution)/shard_map/partial_attend/pallas_call | solution.py:205
  29.9 1.0 %partial_attend.5 = (bf16[16,2560]{1,0:T(8,128)(2,1)S(1)}, bf16[16,2560]{1,0:T(8,128)(2,1)S(1)}, bf16[16,2560]{1,0:T(8,128)(2,1)S(1)}, bf16[16,2560]{1,0:T(8,128...) custom-call(f32[448,128]{1,0:T(8,128)S(1)} %mask_bias.1.bias_ref, ...), custom_call_target="tpu_custom_call" | custom-call | flops 41943040 | bytes 1638400 | tf_op jit(solution)/shard_map/partial_attend/pallas_call | solution.py:205
  30.9 0.1 collective-permute-start.9
  31.0 1.5 %collective-permute-start.12 = (bf16[16,2560]{1,0:T(8,128)(2,1)S(1)}, bf16[16,2560]{1,0:T(8,128)(2,1)S(1)}, u32[]{:S(2)}, u32[]{:S(2)}) collective-permute-start(bf16[16,2560]{1,0:T(8,128)(2,1)S(1)} %get-tuple-element.53), channel_id=1, source_target_pairs={{0,8},{8,24},{24,16},{16,0},{1,9},{9,25},{25,17},{17,1},{2,10},{10... | collective-permute-start | bytes 245768 | tf_op jit(solution)/shard_map/ppermute | solution.py:318
  32.4 0.5 collective-permute-start.15
  33.0 2.0 %collective-permute-start.6 = (bf16[16,2560]{1,0:T(8,128)(2,1)S(1)}, bf16[16,2560]{1,0:T(8,128)(2,1)S(1)}, u32[]{:S(2)}, u32[]{:S(2)}) collective-permute-start(bf16[16,2560]{1,0:T(8,128)(2,1)S(1)} %get-tuple-element.41), channel_id=1, source_target_pairs={{0,8},{8,24},{24,16},{16,0},{1,9},{9,25},{25,17},{17,1},{2,10},{10... | collective-permute-start | bytes 245768 | tf_op jit(solution)/shard_map/ppermute | solution.py:318
  35.0 1.3 %collective-permute-done.9.src_ref = bf16[16,2560]{1,0:T(8,128)(2,1)S(1)} collective-permute-done((bf16[16,2560]{1,0:T(8,128)(2,1)S(1)}, bf16[16,2560]{1,0:T(8,128)(2,1)S(1)}, u32[]{:S(2)}, u32[]{:S(2)}) %collective-permute-start.9) | collective-permute-done | bytes 81952 | tf_op jit(solution)/shard_map/ppermute | solution.py:318
  36.3 1.4 %collective-permute-start.10 = (bf16[16,2560]{1,0:T(8,128)(2,1)S(1)}, bf16[16,2560]{1,0:T(8,128)(2,1)S(1)}, u32[]{:S(2)}, u32[]{:S(2)}) collective-permute-start(bf16[16,2560]{1,0:T(8,128)(2,1)S(1)} %get-tuple-element.49), channel_id=1, source_target_pairs={{8,16},{16,24},{24,0},{0,8},{9,17},{17,25},{25,1},{1,9},{10,18},{1... | collective-permute-start | bytes 245768 | tf_op jit(solution)/shard_map/ppermute | solution.py:318
  37.7 0.4 collective-permute-done.12.src_ref
  38.0 1.4 %collective-permute-start.13 = (bf16[16,2560]{1,0:T(8,128)(2,1)S(1)}, bf16[16,2560]{1,0:T(8,128)(2,1)S(1)}, u32[]{:S(2)}, u32[]{:S(2)}) collective-permute-start(bf16[16,2560]{1,0:T(8,128)(2,1)S(1)} %get-tuple-element.55), channel_id=1, source_target_pairs={{8,16},{16,24},{24,0},{0,8},{9,17},{17,25},{25,1},{1,9},{10,18},{1... | collective-permute-start | bytes 245768 | tf_op jit(solution)/shard_map/ppermute | solution.py:318
  39.4 1.2 %collective-permute-done.15.src_ref = bf16[16,2560]{1,0:T(8,128)(2,1)S(1)} collective-permute-done((bf16[16,2560]{1,0:T(8,128)(2,1)S(1)}, bf16[16,2560]{1,0:T(8,128)(2,1)S(1)}, u32[]{:S(2)}, u32[]{:S(2)}) %collective-permute-start.15) | collective-permute-done | bytes 81952 | tf_op jit(solution)/shard_map/ppermute | solution.py:318
  40.6 0.6 collective-permute-start.16
  41.2 5.7 %collective-permute-done.6.src_ref = bf16[16,2560]{1,0:T(8,128)(2,1)S(1)} collective-permute-done((bf16[16,2560]{1,0:T(8,128)(2,1)S(1)}, bf16[16,2560]{1,0:T(8,128)(2,1)S(1)}, u32[]{:S(2)}, u32[]{:S(2)}) %collective-permute-start.6) | collective-permute-done | bytes 81952 | tf_op jit(solution)/shard_map/ppermute | solution.py:318
  46.9 0.0 collective-permute-start.7
  46.9 0.0 collective-permute-done.10.src_ref
  46.9 0.9 %collective-permute-start.11 = (bf16[16,2560]{1,0:T(8,128)(2,1)S(1)}, bf16[16,2560]{1,0:T(8,128)(2,1)S(1)}, u32[]{:S(2)}, u32[]{:S(2)}) collective-permute-start(bf16[16,2560]{1,0:T(8,128)(2,1)S(1)} %get-tuple-element.51), channel_id=1, source_target_pairs={{16,24},{24,8},{8,0},{0,16},{17,25},{25,9},{9,1},{1,17},{18,26},{2... | collective-permute-start | bytes 245768 | tf_op jit(solution)/shard_map/ppermute | solution.py:318
  47.9 0.0 collective-permute-done.13.src_ref
  47.9 3.9 %collective-permute-start.14 = (bf16[16,2560]{1,0:T(8,128)(2,1)S(1)}, bf16[16,2560]{1,0:T(8,128)(2,1)S(1)}, u32[]{:S(2)}, u32[]{:S(2)}) collective-permute-start(bf16[16,2560]{1,0:T(8,128)(2,1)S(1)} %get-tuple-element.57), channel_id=1, source_target_pairs={{16,24},{24,8},{8,0},{0,16},{17,25},{25,9},{9,1},{1,17},{18,26},{2... | collective-permute-start | bytes 245768 | tf_op jit(solution)/shard_map/ppermute | solution.py:318
  51.8 0.0 collective-permute-done.16.src_ref
  51.8 1.4 %collective-permute-start.17 = (bf16[16,2560]{1,0:T(8,128)(2,1)S(1)}, bf16[16,2560]{1,0:T(8,128)(2,1)S(1)}, u32[]{:S(2)}, u32[]{:S(2)}) collective-permute-start(bf16[16,2560]{1,0:T(8,128)(2,1)S(1)} %get-tuple-element.63), channel_id=1, source_target_pairs={{16,24},{24,8},{8,0},{0,16},{17,25},{25,9},{9,1},{1,17},{18,26},{2... | collective-permute-start | bytes 245768 | tf_op jit(solution)/shard_map/ppermute | solution.py:318
  53.2 0.0 collective-permute-done.7.src_ref
  53.2 1.4 %collective-permute-start.8 = (bf16[16,2560]{1,0:T(8,128)(2,1)S(1)}, bf16[16,2560]{1,0:T(8,128)(2,1)S(1)}, u32[]{:S(2)}, u32[]{:S(2)}) collective-permute-start(bf16[16,2560]{1,0:T(8,128)(2,1)S(1)} %get-tuple-element.45), channel_id=1, source_target_pairs={{16,24},{24,8},{8,0},{0,16},{17,25},{25,9},{9,1},{1,17},{18,26},{2... | collective-permute-start | bytes 245768 | tf_op jit(solution)/shard_map/ppermute | solution.py:318
  54.6 0.0 collective-permute-done.11.src_ref
  54.6 0.0 collective-permute-done.14.src_ref
  54.7 1.6 %collective-permute-done.17.src_ref = bf16[16,2560]{1,0:T(8,128)(2,1)S(1)} collective-permute-done((bf16[16,2560]{1,0:T(8,128)(2,1)S(1)}, bf16[16,2560]{1,0:T(8,128)(2,1)S(1)}, u32[]{:S(2)}, u32[]{:S(2)}) %collective-permute-start.17) | collective-permute-done | bytes 81952 | tf_op jit(solution)/shard_map/ppermute | solution.py:318
  56.3 1.4 %collective-permute-done.8.src_ref = bf16[16,2560]{1,0:T(8,128)(2,1)S(1)} collective-permute-done((bf16[16,2560]{1,0:T(8,128)(2,1)S(1)}, bf16[16,2560]{1,0:T(8,128)(2,1)S(1)}, u32[]{:S(2)}, u32[]{:S(2)}) %collective-permute-start.8) | collective-permute-done | bytes 81952 | tf_op jit(solution)/shard_map/ppermute | solution.py:318
  57.7 0.7 %attend.23 = bf16[64,2560]{1,0:T(8,128)(2,1)} custom-call(f32[448,128]{1,0:T(8,128)S(1)} %mask_bias.1.bias_ref, bf16[16,2560]{1,0:T(8,128)(2,1)S(1)} %collective-permute-done.8.src_ref, f32[1,2560]{1,0:T(1,128)S(1)} %copy-done.1, bf16[2,64,2560]{2,1,0:T(8,128)(2,1)S(1)} %split_kv.5.refs_0_, bf16[2,64,2560]{2,1,0:T(8,128)(2,1)S(1)} %split_kv.4.refs_0_.refs_1_, ...), custom_call_target="tpu_custom_call" | custom-call | flops 73400320 | bytes 4833280 | tf_op jit(solution)/shard_map/attend/pallas_call | solution.py:255
  (15 shorter events, 0.1 us)
Async XLA Ops:
  0.0 16.9 %collective-permute-start = (bf16[64,2,2560]{2,1,0:T(2,128)(2,1)}, bf16[64,2,2560]{2,1,0:T(2,128)(2,1)S(1)}, u32[]{:S(2)}, u32[]{:S(2)}) collective-permute-start(bf16[64,2,2560]{2,1,0:T(2,128)(2,1)} %bitcast.2), channel_id=1, source_target_pairs={{0,1},{7,6},{1,3},{3,5},{5,7},{2,0},{4,2},{6,4},{8,9},{15,14},{9,1... | collective-permute-start | bytes 1966088 | tf_op jit(solution)/shard_map/ppermute | solution.py:275
  0.5 1.1 %copy-start.2 = (bf16[1,64,2,2560]{3,2,1,0:T(2,128)(2,1)S(1)}, bf16[1,64,2,2560]{3,2,1,0:T(2,128)(2,1)}, u32[]{:S(2)}) copy-start(bf16[1,64,2,2560]{3,2,1,0:T(2,128)(2,1)} %param.5) | copy-start | bytes 1966084
  2.0 18.3 %copy-start.3 = (s32[1,7]{1,0:T(1,128)S(1)}, s32[1,7]{1,0:T(1,128)}, u32[]{:S(2)}) copy-start(s32[1,7]{1,0:T(1,128)} %mask_ref.1) | copy-start | bytes 88
  2.0 17.7 %collective-permute-start.2 = (bf16[2,64,2560]{2,1,0:T(8,128)(2,1)S(1)}, bf16[2,64,2560]{2,1,0:T(8,128)(2,1)S(1)}, u32[]{:S(2)}, u32[]{:S(2)}) collective-permute-start(bf16[2,64,2560]{2,1,0:T(8,128)(2,1)S(1)} %split_kv.5.refs_0_), channel_id=1, source_target_pairs={{1,0},{6,7},{3,1},{5,3},{7,5},{0,2},{2,4},{4,6},{9,8},{14,15},{11,... | collective-permute-start | bytes 1966088 | tf_op jit(solution)/shard_map/ppermute | solution.py:275
  4.7 16.2 %collective-permute-start.5 = (bf16[2,64,2560]{2,1,0:T(8,128)(2,1)S(1)}, bf16[2,64,2560]{2,1,0:T(8,128)(2,1)S(1)}, u32[]{:S(2)}, u32[]{:S(2)}) collective-permute-start(bf16[2,64,2560]{2,1,0:T(8,128)(2,1)S(1)} %split_kv.5.refs_0_), channel_id=1, source_target_pairs={{0,1},{1,0},{2,3},{3,2},{4,5},{5,4},{6,7},{7,6},{8,9},{9,8},{10,11... | collective-permute-start | bytes 1966088 | tf_op jit(solution)/shard_map/ppermute | solution.py:275
  16.9 4.0 %copy-start = (bf16[64,2560]{1,0:T(8,128)(2,1)S(1)}, bf16[64,2560]{1,0:T(8,128)(2,1)}, u32[]{:S(2)}) copy-start(bf16[64,2560]{1,0:T(8,128)(2,1)} %src_ref.5) | copy-start | bytes 983044
  17.3 3.6 %copy-start.1 = (f32[1,2560]{1,0:T(1,128)S(1)}, f32[1,2560]{1,0:T(1,128)}, u32[]{:S(2)}) copy-start(f32[1,2560]{1,0:T(1,128)} %gain_ref.29) | copy-start | bytes 30724
  17.3 11.0 %collective-permute-start.1 = (bf16[64,2,2560]{2,1,0:T(2,128)(2,1)S(1)}, bf16[64,2,2560]{2,1,0:T(2,128)(2,1)S(1)}, u32[]{:S(2)}, u32[]{:S(2)}) collective-permute-start(bf16[64,2,2560]{2,1,0:T(2,128)(2,1)S(1)} %collective-permute-done.kv_ref), channel_id=1, source_target_pairs={{0,8},{7,15},{1,2},{3,4},{5,6},{2,1},{4,3},{6,5},{8,0},{15,7},{9,1... | collective-permute-start | bytes 1966088 | tf_op jit(solution)/shard_map/ppermute | solution.py:275
  19.8 9.0 %collective-permute-start.4 = (bf16[2,64,2560]{2,1,0:T(8,128)(2,1)S(1)}, bf16[2,64,2560]{2,1,0:T(8,128)(2,1)S(1)}, u32[]{:S(2)}, u32[]{:S(2)}) collective-permute-start(bf16[2,64,2560]{2,1,0:T(8,128)(2,1)S(1)} %collective-permute-done.2.refs_1_.refs_2_), channel_id=1, source_target_pairs={{0,1},{1,0},{2,3},{3,2},{4,5},{5,4},{6,7},{7,6},{8,9},{9,8},{10,11... | collective-permute-start | bytes 1966088 | tf_op jit(solution)/shard_map/ppermute | solution.py:275
  20.0 8.8 %collective-permute-start.3 = (bf16[2,64,2560]{2,1,0:T(8,128)(2,1)S(1)}, bf16[2,64,2560]{2,1,0:T(8,128)(2,1)S(1)}, u32[]{:S(2)}, u32[]{:S(2)}) collective-permute-start(bf16[2,64,2560]{2,1,0:T(8,128)(2,1)S(1)} %split_kv.4.refs_0_.refs_1_), channel_id=1, source_target_pairs={{0,1},{1,0},{2,3},{3,2},{4,5},{5,4},{6,7},{7,6},{8,9},{9,8},{10,11... | collective-permute-start | bytes 1966088 | tf_op jit(solution)/shard_map/ppermute | solution.py:275
  30.9 5.4 %collective-permute-start.9 = (bf16[16,2560]{1,0:T(8,128)(2,1)S(1)}, bf16[16,2560]{1,0:T(8,128)(2,1)S(1)}, u32[]{:S(2)}, u32[]{:S(2)}) collective-permute-start(bf16[16,2560]{1,0:T(8,128)(2,1)S(1)} %get-tuple-element.47), channel_id=1, source_target_pairs={{0,8},{8,24},{24,16},{16,0},{1,9},{9,25},{25,17},{17,1},{2,10},{10... | collective-permute-start | bytes 245768 | tf_op jit(solution)/shard_map/ppermute | solution.py:318
  31.0 7.1 %collective-permute-start.12 = (bf16[16,2560]{1,0:T(8,128)(2,1)S(1)}, bf16[16,2560]{1,0:T(8,128)(2,1)S(1)}, u32[]{:S(2)}, u32[]{:S(2)}) collective-permute-start(bf16[16,2560]{1,0:T(8,128)(2,1)S(1)} %get-tuple-element.53), channel_id=1, source_target_pairs={{0,8},{8,24},{24,16},{16,0},{1,9},{9,25},{25,17},{17,1},{2,10},{10... | collective-permute-start | bytes 245768 | tf_op jit(solution)/shard_map/ppermute | solution.py:318
  32.4 8.2 %collective-permute-start.15 = (bf16[16,2560]{1,0:T(8,128)(2,1)S(1)}, bf16[16,2560]{1,0:T(8,128)(2,1)S(1)}, u32[]{:S(2)}, u32[]{:S(2)}) collective-permute-start(bf16[16,2560]{1,0:T(8,128)(2,1)S(1)} %get-tuple-element.59), channel_id=1, source_target_pairs={{0,8},{8,24},{24,16},{16,0},{1,9},{9,25},{25,17},{17,1},{2,10},{10... | collective-permute-start | bytes 245768 | tf_op jit(solution)/shard_map/ppermute | solution.py:318
  33.0 13.9 %collective-permute-start.6 = (bf16[16,2560]{1,0:T(8,128)(2,1)S(1)}, bf16[16,2560]{1,0:T(8,128)(2,1)S(1)}, u32[]{:S(2)}, u32[]{:S(2)}) collective-permute-start(bf16[16,2560]{1,0:T(8,128)(2,1)S(1)} %get-tuple-element.41), channel_id=1, source_target_pairs={{0,8},{8,24},{24,16},{16,0},{1,9},{9,25},{25,17},{17,1},{2,10},{10... | collective-permute-start | bytes 245768 | tf_op jit(solution)/shard_map/ppermute | solution.py:318
  36.3 10.6 %collective-permute-start.10 = (bf16[16,2560]{1,0:T(8,128)(2,1)S(1)}, bf16[16,2560]{1,0:T(8,128)(2,1)S(1)}, u32[]{:S(2)}, u32[]{:S(2)}) collective-permute-start(bf16[16,2560]{1,0:T(8,128)(2,1)S(1)} %get-tuple-element.49), channel_id=1, source_target_pairs={{8,16},{16,24},{24,0},{0,8},{9,17},{17,25},{25,1},{1,9},{10,18},{1... | collective-permute-start | bytes 245768 | tf_op jit(solution)/shard_map/ppermute | solution.py:318
  38.0 9.8 %collective-permute-start.13 = (bf16[16,2560]{1,0:T(8,128)(2,1)S(1)}, bf16[16,2560]{1,0:T(8,128)(2,1)S(1)}, u32[]{:S(2)}, u32[]{:S(2)}) collective-permute-start(bf16[16,2560]{1,0:T(8,128)(2,1)S(1)} %get-tuple-element.55), channel_id=1, source_target_pairs={{8,16},{16,24},{24,0},{0,8},{9,17},{17,25},{25,1},{1,9},{10,18},{1... | collective-permute-start | bytes 245768 | tf_op jit(solution)/shard_map/ppermute | solution.py:318
  40.6 11.2 %collective-permute-start.16 = (bf16[16,2560]{1,0:T(8,128)(2,1)S(1)}, bf16[16,2560]{1,0:T(8,128)(2,1)S(1)}, u32[]{:S(2)}, u32[]{:S(2)}) collective-permute-start(bf16[16,2560]{1,0:T(8,128)(2,1)S(1)} %get-tuple-element.61), channel_id=1, source_target_pairs={{8,16},{16,24},{24,0},{0,8},{9,17},{17,25},{25,1},{1,9},{10,18},{1... | collective-permute-start | bytes 245768 | tf_op jit(solution)/shard_map/ppermute | solution.py:318
  46.9 6.4 %collective-permute-start.7 = (bf16[16,2560]{1,0:T(8,128)(2,1)S(1)}, bf16[16,2560]{1,0:T(8,128)(2,1)S(1)}, u32[]{:S(2)}, u32[]{:S(2)}) collective-permute-start(bf16[16,2560]{1,0:T(8,128)(2,1)S(1)} %get-tuple-element.43), channel_id=1, source_target_pairs={{8,16},{16,24},{24,0},{0,8},{9,17},{17,25},{25,1},{1,9},{10,18},{1... | collective-permute-start | bytes 245768 | tf_op jit(solution)/shard_map/ppermute | solution.py:318
  46.9 7.7 %collective-permute-start.11 = (bf16[16,2560]{1,0:T(8,128)(2,1)S(1)}, bf16[16,2560]{1,0:T(8,128)(2,1)S(1)}, u32[]{:S(2)}, u32[]{:S(2)}) collective-permute-start(bf16[16,2560]{1,0:T(8,128)(2,1)S(1)} %get-tuple-element.51), channel_id=1, source_target_pairs={{16,24},{24,8},{8,0},{0,16},{17,25},{25,9},{9,1},{1,17},{18,26},{2... | collective-permute-start | bytes 245768 | tf_op jit(solution)/shard_map/ppermute | solution.py:318
  47.9 6.8 %collective-permute-start.14 = (bf16[16,2560]{1,0:T(8,128)(2,1)S(1)}, bf16[16,2560]{1,0:T(8,128)(2,1)S(1)}, u32[]{:S(2)}, u32[]{:S(2)}) collective-permute-start(bf16[16,2560]{1,0:T(8,128)(2,1)S(1)} %get-tuple-element.57), channel_id=1, source_target_pairs={{16,24},{24,8},{8,0},{0,16},{17,25},{25,9},{9,1},{1,17},{18,26},{2... | collective-permute-start | bytes 245768 | tf_op jit(solution)/shard_map/ppermute | solution.py:318
  51.8 4.5 %collective-permute-start.17 = (bf16[16,2560]{1,0:T(8,128)(2,1)S(1)}, bf16[16,2560]{1,0:T(8,128)(2,1)S(1)}, u32[]{:S(2)}, u32[]{:S(2)}) collective-permute-start(bf16[16,2560]{1,0:T(8,128)(2,1)S(1)} %get-tuple-element.63), channel_id=1, source_target_pairs={{16,24},{24,8},{8,0},{0,16},{17,25},{25,9},{9,1},{1,17},{18,26},{2... | collective-permute-start | bytes 245768 | tf_op jit(solution)/shard_map/ppermute | solution.py:318
  53.2 4.5 %collective-permute-start.8 = (bf16[16,2560]{1,0:T(8,128)(2,1)S(1)}, bf16[16,2560]{1,0:T(8,128)(2,1)S(1)}, u32[]{:S(2)}, u32[]{:S(2)}) collective-permute-start(bf16[16,2560]{1,0:T(8,128)(2,1)S(1)} %get-tuple-element.45), channel_id=1, source_target_pairs={{16,24},{24,8},{8,0},{0,16},{17,25},{25,9},{9,1},{1,17},{18,26},{2... | collective-permute-start | bytes 245768 | tf_op jit(solution)/shard_map/ppermute | solution.py:318
